TPU v7x, 256 devices: a whole 4x4x8 slice. The times are simulated.
256 devices in a mesh: blk: 16 (over x_lo, y, core), mod: 16 (over x_hi, z).
Axes of the slice: x: 4 (x_hi: 2, x_lo: 2; x = x_hi * 2 + x_lo), y: 4, z: 8, core: 2. Of those that a mesh axis runs over, the one named last changes fastest.
Arguments:
- act: bfloat16 [16, 32, 16384], P('mod', None, 'blk'), may hold values from -6 to 6
- grad: bfloat16 [16, 64, 16384], P('mod', None, 'blk'), may hold values from -40 to 40
- train: bfloat16 [16, 32768, 2048], P('mod', 'blk'), may hold values from -24 to 24
- pre_out: float32 [16, 64, 64], P('mod'), may hold values from -0.75 to 0.75
- pre_in: float32 [16, 32, 32], P('mod'), may hold values from -1 to 1
- doc_ids: int32 [16384, 1], P('blk'), may hold values from 0 to 511; in each aligned block of 1024 rows (0 to 1023, 1024 to 2047, ...) at most 4 rows name the same one
- owners: int32 [512], replicated, may hold values from 0 to 511, each once
Outputs:
- scores: float32 [16, 512, 32768], P('mod', None, 'blk')
Inputs may be any that keep to these rules, and one draw needn't show every extreme that they name: `doc_ids`: among the 1024 tokens of one index of blk no document has more than 4 tokens, and some document has exactly 4 in some such block; every document has at least one token. `owners`: A permutation of the 512 documents.
All inputs are finite; a program needn't handle non-finite values.
Results may differ from a plain program's by a relative error of at most 0.0029.
Values may be sent and summed in bfloat16 or wider, within the bound.
No kernel may reach another device: no remote copies, remote signals or barrier semaphores. Data moves between devices by JAX's collectives and lax.ppermute only.
A program may use at most 64 MiB of HBM per device.

v0:
```python
import jax
import jax.numpy as jnp
from jax import lax
from jax.sharding import PartitionSpec as P

A = 32
G = 64
MOST = 4


def place_tokens(doc_index, owners):
    doc_count = owners.shape[0]
    matches = (doc_index[:, None] == owners[None, :]).astype(jnp.int32)
    position = jnp.sum(matches * jnp.arange(doc_count, dtype=jnp.int32)[None, :], axis=1)
    ordinal = jnp.arange(doc_index.shape[0], dtype=jnp.int32)
    earlier = (doc_index[:, None] == doc_index[None, :]) & (ordinal[None, :] < ordinal[:, None])
    rank_in_doc = jnp.sum(earlier.astype(jnp.int32), axis=1)
    return (position, rank_in_doc)


def condition(doc_grads, pre_out, pre_in):
    left = jnp.einsum("hg,kga->kha", pre_out[0], doc_grads, precision=lax.Precision.HIGHEST)
    return jnp.einsum("kha,ab->khb", left, pre_in[0], precision=lax.Precision.HIGHEST)


def body(act, grad, train, pre_out, pre_in, doc_ids, owners):
    blocks = lax.axis_size("blk")
    doc_count = owners.shape[0]
    per_owner = doc_count // blocks
    width = A + G
    token_rows = jnp.concatenate([act[0], grad[0]], axis=0)
    train_rows = train[0]
    position, rank_in_doc = place_tokens(doc_ids[:, 0], owners)
    slot = position * MOST + rank_in_doc
    send_buffer = jnp.zeros((width, doc_count * MOST), jnp.bfloat16).at[:, slot].set(token_rows)
    received = lax.all_to_all(
        send_buffer.reshape(width, blocks, per_owner * MOST),
        "blk",
        split_axis=1,
        concat_axis=1,
        tiled=True,
    )
    slots = received.reshape(width, blocks, per_owner, MOST)
    doc_grads = jnp.einsum(
        "gskm,askm->kga", slots[A:], slots[:A], preferred_element_type=jnp.float32
    )
    cond = condition(doc_grads, pre_out, pre_in)
    local_squares = jnp.sum(cond * cond, axis=(1, 2))
    total_squares = lax.psum(local_squares, "mod")
    inverse = 1.0 / jnp.sqrt(total_squares + 1e-06)
    doc_b = (cond.reshape(per_owner, G * A) * inverse[:, None]).astype(jnp.bfloat16)
    result = lax.dot_general(
        lax.all_gather(doc_b, "blk", axis=0, tiled=True),
        train_rows,
        (((1,), (1,)), ((), ())),
        preferred_element_type=jnp.float32,
    )
    return result[None]


def solution(mesh):
    return jax.shard_map(
        body,
        mesh=mesh,
        in_specs=(
            P("mod", None, "blk"),
            P("mod", None, "blk"),
            P("mod", "blk", None),
            P("mod", None, None),
            P("mod", None, None),
            P("blk", None),
            P(),
        ),
        out_specs=P("mod", None, "blk"),
        check_vma=False,
    )
```

profile of v0, /device:TPU:1, one launch (start us, length us, event | category | flops | bytes accessed | tf_op | source)
XLA Modules:
  0.0 124.8 jit_solution(13324611681313143171)
XLA Ops:
  6.5 0.0 copy-start
  6.5 0.0 copy-start.1
  6.5 0.0 all-gather.2.cloned.1.call-start
  6.5 1.3 %convert_reduce_fusion = s32[1024]{0:T(1024)S(1)} fusion(s32[1024]{0:T(1024)} %bitcast.45), kind=kLoop, calls=%fused_computation.3 | loop fusion | flops 5241856 | bytes 8192 | tf_op jit(solution)/shard_map/reduce_sum | solution.py:17
  7.8 1.1 select_reduce_fusion
  9.0 0.9 maximum_bitcast_fusion
  9.9 0.2 copy.19
  10.1 3.3 %scatter_custom_fusion = bf16[96,2048]{0,1:T(8,128)(2,1)S(1)} fusion(s32[1024]{0:T(1024)S(1)} %bitcast.47, bf16[1024,96]{1,0:T(8,128)(2,1)S(1)} %copy.19, bf16[]{:T(256)} %constant.6.clone.1), kind=kCustom, calls=%fused_computation.12 | custom fusion | bytes 393218 | tf_op jit(solution)/shard_map/scatter | solution.py:35
  13.5 0.3 copy.20
  13.7 15.1 %all_to_all.5 = bf16[96,16,128]{2,0,1:T(8,128)(2,1)S(1)} all-to-all(bf16[96,16,128]{2,0,1:T(8,128)(2,1)S(1)} %copy.20), channel_id=1, replica_groups=mesh['blk'=16,'mod'=16] {'blk'}, dimensions={1} | all-to-all | bytes 786432 | tf_op jit(solution)/shard_map/all_to_all | solution.py:36
  28.8 0.4 copy.21
  29.3 0.4 copy.22
  29.7 0.3 convolution_bitcast_fusion.1
  30.1 0.0 copy-done
  30.1 0.6 convolution_bitcast_fusion
  30.6 0.0 copy-done.1
  30.6 0.9 multiply_reduce_fusion
  31.5 37.4 %psum.7 = f32[32]{0:T(128)S(1)} all-reduce(f32[32]{0:T(128)S(1)} %get-tuple-element.5), channel_id=1, replica_groups=mesh['blk'=16,'mod'=16] {'mod'}, use_global_device_ids=true, to_apply=%region_4.0 | all-reduce | flops 32 | bytes 256 | tf_op jit(solution)/shard_map/psum | solution.py:49
  69.0 0.4 copy.24
  69.3 0.5 reshape.39
  69.8 0.7 multiply_convert_fusion
  70.6 0.0 all-gather.2.cloned.1.call-update
  70.6 36.8 %all-gather.2.cloned.1.call-done = bf16[512,2048]{1,0:T(8,128)(2,1)} async-done(((bf16[32,2048]{1,0:T(8,128)(2,1)}), bf16[512,2048]{1,0:T(8,128)(2,1)}) %all-gather.2.cloned.1.call-update) | async-done | bytes 2097168 | tf_op jit(solution)/shard_map/all_gather | solution.py:53
  107.4 10.6 %fusion.3 = f32[1,512,2048]{2,1,0:T(8,128)} fusion(bf16[512,2048]{1,0:T(8,128)(2,1)} %all-gather.2.cloned.1.call-done, bf16[1,2048,2048]{2,1,0:T(8,128)(2,1)} %param.9), kind=kOutput, calls=%fused_computation.6 | convolution fusion | flops 4294967296 | bytes 14680064 | tf_op jit(solution)/shard_map/dot_general | solution.py:52
  (5 shorter events, 0.0 us)
Async XLA Ops:
  6.5 23.5 %copy-start = (f32[1,64,64]{2,1,0:T(8,128)S(1)}, f32[1,64,64]{2,1,0:T(8,128)}, u32[]{:S(2)}) copy-start(f32[1,64,64]{2,1,0:T(8,128)} %param.10) | copy-start | bytes 49156
  6.5 24.1 %copy-start.1 = (f32[1,32,32]{2,1,0:T(8,128)S(1)}, f32[1,32,32]{2,1,0:T(8,128)}, u32[]{:S(2)}) copy-start(f32[1,32,32]{2,1,0:T(8,128)} %param.11) | copy-start | bytes 12292
  6.5 100.8 %all-gather.2.cloned.1.call-start = ((), (), s32[]{:S(2)}) async-start(), calls=%async_computation.1 | async-start | bytes 2228224 | tf_op jit(solution)/shard_map/all_gather | solution.py:53
Sparse Core Ops, SparseCore 0:
  70.7 36.5 all-gather.1
where the time goes:
time: 125 us
  blocking collectives  52.5 us (42%)
  waiting for transfers between devices  36.8 us (29%)
  between operations  13.5 us (11%)
  matrix products  12.3 us (10%)
  local copies, waits for them, and re-layouts  5.52 us (4%)
  other arithmetic  4.11 us (3%)
    psum x1, blocking collectives, body(): total_squares = lax.psum(local_squares, 'mod')  37.4 us
    all_gather x1, waiting for transfers between devices, body(): lax.all_gather(doc_b, 'blk', axis=0, tiled=True)  36.8 us
    all_to_all x1, blocking collectives, body(): lax.all_to_all(send_buffer.reshape(width, blocks, per_owner * MOST), 'blk...  15.1 us
    dot_general x1, matrix products, body(): lax.dot_general(lax.all_gather(doc_b, 'blk', axis=0, tiled=True), train_r...  10.6 us
    scatter x1, local copies, waits for them, and re-layouts, body(): jnp.zeros((width, doc_count * MOST), jnp.bfloat16).at[:, slot]  3.34 us
  transfers between devices with their start and end apart: 1, of which 1 were waited for; matrix products, arithmetic and copies ran while one was open for 0% of the time, Pallas kernels for 0%

commit v1 on v0

v1 whole, which is shorter than its diff:
```python
import functools

import jax
import jax.numpy as jnp
from jax import lax
from jax.experimental import pallas as pl
from jax.experimental.pallas import tpu as pltpu
from jax.sharding import Mesh, PartitionSpec as P

A = 32
G = 64
W = A + G
MOST = 4
BLK = 16
OWN = 32
DOCS = 512
TOK = 1024
LANES = OWN * MOST
F = G * A
BF = jnp.bfloat16
F32 = jnp.float32
NT = (((1,), (1,)), ((), ()))
BLK_AXES = ("xl", "y", "core")
MOD_AXES = ("xh", "z")
VM = pl.BlockSpec(memory_space=pltpu.VMEM)


def iota(shape, axis):
    return lax.broadcasted_iota(jnp.int32, shape, axis)


def slot_kernel(act_ref, grad_ref, ids_ref, own_ref, send_ref):
    ids = ids_ref[...]
    ids_col = jnp.transpose(jnp.broadcast_to(ids, (8, TOK)))[:, :1]
    own_col = jnp.transpose(jnp.broadcast_to(own_ref[...], (8, DOCS)))[:, :1]
    place = jnp.sum(jnp.where(own_col == ids, iota((DOCS, TOK), 0), 0), axis=0, keepdims=True)
    step = 128
    ranks = []
    for j in range(TOK // step):
        mine = ids[:, j * step : (j + 1) * step]
        there = ids_col[j * step : (j + 1) * step]
        same = (there == mine) & (iota((step, step), 0) < iota((step, step), 1))
        count = jnp.sum(same.astype(jnp.int32), axis=0, keepdims=True)
        if j:
            count += jnp.sum((ids_col[: j * step] == mine).astype(jnp.int32), axis=0, keepdims=True)
        ranks.append(count)
    slot = place * MOST + jnp.concatenate(ranks, axis=1)
    group = slot // 256
    inner = slot % 256
    hot = (iota((256, TOK), 0) == inner).astype(F32).astype(BF)
    rows = jnp.concatenate([act_ref[0], grad_ref[0]], axis=0)
    zero = jnp.zeros_like(rows)
    for o in range(BLK // 2):
        part = jnp.where(group == o, rows, zero)
        got = lax.dot_general(part, hot, NT, preferred_element_type=F32).astype(BF)
        send_ref[2 * o] = got[:, :LANES]
        send_ref[2 * o + 1] = got[:, LANES:]


def split(x):
    hi = x.astype(BF)
    return hi, (x - hi.astype(F32)).astype(BF)


def dot(a, b):
    return jnp.dot(a, b, preferred_element_type=F32)


def cond_kernel(recv_ref, po_ref, pi_ref, cond_ref, square_ref):
    doc = jnp.zeros((G, OWN * A), F32)
    mask = (iota((OWN * A, LANES), 0) // A) == (iota((OWN * A, LANES), 1) // MOST)
    wide = jnp.concatenate([mask, mask], axis=1)
    for s in range(0, BLK, 2):
        act = jnp.concatenate([recv_ref[s, :A], recv_ref[s + 1, :A]], axis=1)
        grad = jnp.concatenate([recv_ref[s, A:], recv_ref[s + 1, A:]], axis=1)
        spread = jnp.concatenate([act] * OWN, axis=0)
        spread = jnp.where(wide, spread, jnp.zeros_like(spread))
        doc += lax.dot_general(grad, spread, NT, preferred_element_type=F32)
    po_hi, po_lo = split(po_ref[0])
    d_hi, d_lo = split(doc)
    left = dot(
        jnp.concatenate([po_hi, po_hi, po_lo, po_lo], axis=1),
        jnp.concatenate([d_hi, d_lo, d_hi, d_lo], axis=0),
    )
    pick = (iota((A, 256), 0) == iota((A, 256), 1) % A).astype(F32).astype(BF)
    diag = (iota((256, 256), 0) // A) == (iota((256, 256), 1) // A)

    def block_diagonal(part):
        row = dot(part, pick)
        full = jnp.concatenate([row] * 8, axis=0)
        return jnp.where(diag, full, 0.0).astype(BF)

    pi_hi, pi_lo = split(pi_ref[0])
    pi_hi, pi_lo = block_diagonal(pi_hi), block_diagonal(pi_lo)
    l_hi, l_lo = split(left)
    outs = []
    for q in range(OWN * A // 256):
        cols = slice(q * 256, (q + 1) * 256)
        outs.append(dot(l_hi[:, cols], pi_hi) + dot(l_lo[:, cols], pi_hi) + dot(l_hi[:, cols], pi_lo))
    cond = jnp.concatenate(outs, axis=1)
    cond = jnp.transpose(cond.reshape(G, OWN, A), (1, 0, 2)).reshape(OWN, F)
    cond_ref[...] = cond
    square = jnp.sum(cond * cond, axis=1, keepdims=True)
    row = jnp.transpose(jnp.broadcast_to(square, (OWN, 128)))[:8]
    row = jnp.concatenate([row, jnp.zeros((8, 128 - OWN), F32)], axis=1)
    for m in range(BLK):
        square_ref[m] = row


def scale_kernel(cond_ref, squares_ref, doc_ref):
    total = jnp.sum(squares_ref[...], axis=0)
    inverse = 1.0 / jnp.sqrt(total + 1e-6)
    inverse = jnp.transpose(jnp.broadcast_to(inverse[:1], (8, 128)))[:OWN, :1]
    doc_ref[...] = (cond_ref[...] * inverse).astype(BF)


def score_kernel(count, from_ref, *refs):
    blocks, train_ref, out_ref, docs_ref = refs[:count], refs[count], refs[count + 1], refs[count + 2]

    @pl.when(pl.program_id(0) == 0)
    def _():
        for i in range(count):
            at = pl.multiple_of(from_ref[i] * OWN, OWN)
            docs_ref[pl.ds(at, OWN), :] = blocks[i][...]

    out_ref[0] = lax.dot_general(docs_ref[...], train_ref[0], NT, preferred_element_type=F32)


def swap(x, axis):
    return lax.ppermute(x, axis, [(0, 1), (1, 0)])


def turn(x, by):
    return lax.ppermute(x, "y", [(i, (i + by) % 4) for i in range(4)])


def gather_docs(doc):
    x, y, c = (lax.axis_index(a) for a in BLK_AXES)

    def source(dx, dy, dc):
        return ((x ^ dx) * 4 + (y + dy) % 4) * 2 + (c ^ dc)

    half = OWN // 2
    got = {(0, 0): doc}
    got[1, 0] = swap(doc, "xl")
    got[0, 3] = turn(doc, 1)
    got[0, 1] = turn(doc, -1)
    got[1, 3] = swap(got[0, 3], "xl")
    got[0, 2] = turn(got[0, 3], 1)
    got[1, 1] = turn(got[1, 0], -1)
    last = [swap(got[0, 2][:half], "xl"), turn(got[1, 1][half:], -1)]
    mates = {k: swap(v, "core") for k, v in got.items()}
    got[1, 2] = jnp.concatenate(last, axis=0)
    mates[1, 2] = jnp.concatenate([swap(v, "core") for v in last], axis=0)
    blocks = [*got.values(), *mates.values()]
    places = [source(*k, 0) for k in got] + [source(*k, 1) for k in mates]
    return blocks, jnp.stack(places).astype(jnp.int32)


def body(act, grad, train, pre_out, pre_in, doc_ids, owners):
    send = pl.pallas_call(
        slot_kernel,
        out_shape=jax.ShapeDtypeStruct((BLK, W, LANES), BF),
        in_specs=[VM] * 4,
        out_specs=VM,
        name="slots",
    )(act, grad, doc_ids.reshape(1, TOK), owners.reshape(1, DOCS))
    received = lax.all_to_all(send, BLK_AXES, split_axis=0, concat_axis=0, tiled=True)
    cond, squares = pl.pallas_call(
        cond_kernel,
        out_shape=(
            jax.ShapeDtypeStruct((OWN, F), F32),
            jax.ShapeDtypeStruct((BLK, 8, 128), F32),
        ),
        in_specs=[VM] * 3,
        out_specs=(VM, VM),
        name="condition",
    )(received, pre_out, pre_in)
    squares = lax.all_to_all(squares, MOD_AXES, split_axis=0, concat_axis=0, tiled=True)
    doc = pl.pallas_call(
        scale_kernel,
        out_shape=jax.ShapeDtypeStruct((OWN, F), BF),
        in_specs=[VM] * 2,
        out_specs=VM,
        name="scale",
    )(cond, squares)
    blocks, places = gather_docs(doc)
    tile = 256
    rows = train.shape[1]
    return pl.pallas_call(
        functools.partial(score_kernel, len(blocks)),
        out_shape=jax.ShapeDtypeStruct((1, DOCS, rows), F32),
        grid_spec=pltpu.PrefetchScalarGridSpec(
            num_scalar_prefetch=1,
            grid=(rows // tile,),
            in_specs=[VM] * len(blocks) + [pl.BlockSpec((1, tile, F), lambda i, s: (0, i, 0))],
            out_specs=pl.BlockSpec((1, DOCS, tile), lambda i, s: (0, 0, i)),
            scratch_shapes=[pltpu.VMEM((DOCS, F), BF)],
        ),
        name="scores",
    )(places, *blocks, train)


def solution(mesh):
    fine = Mesh(mesh.devices.reshape(2, 4, 2, 2, 8), (*BLK_AXES, *MOD_AXES))
    return jax.shard_map(
        body,
        mesh=fine,
        in_specs=(
            P(MOD_AXES, None, BLK_AXES),
            P(MOD_AXES, None, BLK_AXES),
            P(MOD_AXES, BLK_AXES, None),
            P(MOD_AXES, None, None),
            P(MOD_AXES, None, None),
            P(BLK_AXES, None),
            P(),
        ),
        out_specs=P(MOD_AXES, None, BLK_AXES),
        check_vma=False,
    )
```

time: 125 us -> 85.4 us (0.68)
  waiting for transfers between devices: 36.8 us -> 10.1 us
  Pallas kernels: 0 us -> 21.4 us
  blocking collectives: 52.5 us -> 34.8 us
  starting transfers between devices: 0.01 us -> 15.1 us
  between operations: 13.5 us -> 0.16 us
  matrix products: 12.3 us -> 0 us
  local copies, waits for them, and re-layouts: 5.52 us -> 1.97 us
  other arithmetic: 4.11 us -> 1.33 us
    psum x1 -> x0, blocking collectives: 37.4 us -> none  [body(): total_squares = lax.psum(local_squares, 'mod')]
    all_gather x1 -> x0, waiting for transfers between devices: 36.8 us -> none  [body(): lax.all_gather(doc_b, 'blk', axis=0, tiled=True)]
    pallas_call x0 -> x4, Pallas kernels: none -> 21.4 us  [the longest x1 11.8 us: body(): pl.pallas_call(functools.partial(score_kernel, len(blocks)), out_shape=ja...]
    all_to_all x1 -> x2, blocking collectives: 15.1 us -> 34.8 us  [the longest x1 19.1 us: body(): lax.all_to_all(squares, MOD_AXES, split_axis=0, concat_axis=0, tiled=True)]
    ppermute x0 -> x17, starting transfers between devices: none -> 15.1 us  [the longest x12 9.86 us: swap(): return lax.ppermute(x, axis, [(0, 1), (1, 0)])]
    dot_general x4 -> x0, matrix products: 12.3 us -> none  [the longest x1 10.6 us: body(): lax.dot_general(lax.all_gather(doc_b, 'blk', axis=0, tiled=True), train_r...]
    ppermute x0 -> x17, waiting for transfers between devices: none -> 10.1 us  [the longest x5 7.08 us: turn(): return lax.ppermute(x, 'y', [(i, (i + by) % 4) for i in range(4)])]
    scatter x1 -> x0, local copies, waits for them, and re-layouts: 3.34 us -> none  [body(): jnp.zeros((width, doc_count * MOST), jnp.bfloat16).at[:, slot]]
  transfers between devices with their start and end apart: 1 -> 17, of which waited for: 1 -> 4; matrix products, arithmetic and copies ran while one was open for 0% -> 2% of each run, Pallas kernels for 0% -> 0%
where the time goes in v1:
time: 85.4 us; the launch traced here: 84.9 us
  blocking collectives  34.8 us (41%)
  Pallas kernels  21.4 us (25%)
  starting transfers between devices  15.1 us (18%)
  waiting for transfers between devices  10.1 us (12%)
  local copies, waits for them, and re-layouts  1.97 us (2%)
  other arithmetic  1.33 us (2%)
    all_to_all x1, blocking collectives, body(): lax.all_to_all(squares, MOD_AXES, split_axis=0, concat_axis=0, tiled=True)  19.1 us
    all_to_all x1, blocking collectives, body(): lax.all_to_all(send, BLK_AXES, split_axis=0, concat_axis=0, tiled=True)  15.7 us
    pallas_call x1, Pallas kernels, body(): pl.pallas_call(functools.partial(score_kernel, len(blocks)), out_shape=ja...  11.8 us
    ppermute x12, starting transfers between devices, swap(): return lax.ppermute(x, axis, [(0, 1), (1, 0)])  9.86 us
    ppermute x5, waiting for transfers between devices, turn(): return lax.ppermute(x, 'y', [(i, (i + by) % 4) for i in range(4)])  7.08 us
    ppermute x5, starting transfers between devices, turn(): return lax.ppermute(x, 'y', [(i, (i + by) % 4) for i in range(4)])  5.19 us
    pallas_call x1, Pallas kernels, body(): pl.pallas_call(cond_kernel, out_shape=(jax.ShapeDtypeStruct((OWN, F), F32...  4.1 us
    pallas_call x1, Pallas kernels, body(): pl.pallas_call(slot_kernel, out_shape=jax.ShapeDtypeStruct((BLK, W, LANES...  3.79 us
  transfers between devices with their start and end apart: 17, of which 4 were waited for; matrix products, arithmetic and copies ran while one was open for 2% of the time, Pallas kernels for 0%

profile of v1, /device:TPU:1, one launch (start us, length us, event | category | flops | bytes accessed | tf_op | source)
XLA Modules:
  0.0 84.9 jit_solution(13373013318932049102)
XLA Ops:
  0.0 3.8 %slots.1 = bf16[16,96,128]{2,1,0:T(8,128)(2,1)} custom-call(bf16[1,32,1024]{2,1,0:T(8,128)(2,1)} %act_ref.1, bf16[1,64,1024]{2,1,0:T(8,128)(2,1)} %grad_ref.1, s32[1,1024]{1,0:T(1,128)} %bitcast.18, s32[1,512]{1,0:T(1,128)} %bitcast.19), custom_call_target="tpu_custom_call" | custom-call | tf_op jit(solution)/shard_map/slots/pallas_call | solution.py:161
  3.8 15.7 %all_to_all.10.recv_ref = bf16[16,96,128]{2,1,0:T(8,128)(2,1)} all-to-all(bf16[16,96,128]{2,1,0:T(8,128)(2,1)} %slots.1), channel_id=1, replica_groups=mesh['xl'=2,'y'=4,'core'=2,'xh'=2,'z'=8] {'xl','y','core'}, dimensions={0} | all-to-all | bytes 786432 | tf_op jit(solution)/shard_map/all_to_all | solution.py:168
  19.5 4.1 %condition.1 = (f32[32,2048]{1,0:T(8,128)}, f32[16,8,128]{2,1,0:T(8,128)}) custom-call(bf16[16,96,128]{2,1,0:T(8,128)(2,1)} %all_to_all.10.recv_ref, f32[1,64,64]{2,1,0:T(8,128)} %po_ref.1, f32[1,32,32]{2,1,0:T(8,128)} %pi_ref.1), custom_call_target="tpu_custom_call" | custom-call | tf_op jit(solution)/shard_map/condition/pallas_call | solution.py:169
  23.6 19.1 %all_to_all.11.squares_ref = f32[16,8,128]{2,1,0:T(8,128)} all-to-all(f32[16,8,128]{2,1,0:T(8,128)} %get-tuple-element.8), channel_id=1, replica_groups=mesh['xl'=2,'y'=4,'core'=2,'xh'=2,'z'=8] {'xh','z'}, dimensions={0} | all-to-all | bytes 131072 | tf_op jit(solution)/shard_map/all_to_all | solution.py:179
  42.7 1.8 %scale.1.refs_0_ = bf16[32,2048]{1,0:T(8,128)(2,1)} custom-call(f32[32,2048]{1,0:T(8,128)} %get-tuple-element.7.cond_ref, f32[16,8,128]{2,1,0:T(8,128)} %all_to_all.11.squares_ref), custom_call_target="tpu_custom_call" | custom-call | tf_op jit(solution)/shard_map/scale/pallas_call | solution.py:180
  44.5 0.0 collective-permute-start.1
  44.5 0.4 collective-permute-start
  45.0 4.8 %collective-permute-done.1.refs_2_ = bf16[32,2048]{1,0:T(8,128)(2,1)S(1)} collective-permute-done((bf16[32,2048]{1,0:T(8,128)(2,1)}, bf16[32,2048]{1,0:T(8,128)(2,1)S(1)}, u32[]{:S(2)}, u32[]{:S(2)}) %collective-permute-start.1) | collective-permute-done | bytes 131104 | tf_op jit(solution)/shard_map/ppermute | solution.py:134
  49.8 0.0 collective-permute-start.4
  49.8 0.0 collective-permute-done.refs_1_
  49.8 2.7 %collective-permute-start.5 = (bf16[32,2048]{1,0:T(8,128)(2,1)S(1)}, bf16[32,2048]{1,0:T(8,128)(2,1)S(1)}, u32[]{:S(2)}, u32[]{:S(2)}) collective-permute-start(bf16[32,2048]{1,0:T(8,128)(2,1)S(1)} %collective-permute-done.refs_1_), channel_id=1, source_target_pairs={{0,96},{32,0},{64,32},{96,64},{1,97},{33,1},{65,33},{97,65},{2,98}... | collective-permute-start | bytes 393224 | tf_op jit(solution)/shard_map/ppermute | solution.py:134
  52.4 0.1 collective-permute-start.2
  52.5 2.3 %collective-permute-done.4.refs_5_ = bf16[32,2048]{1,0:T(8,128)(2,1)S(1)} collective-permute-done((bf16[32,2048]{1,0:T(8,128)(2,1)S(1)}, bf16[32,2048]{1,0:T(8,128)(2,1)S(1)}, u32[]{:S(2)}, u32[]{:S(2)}) %collective-permute-start.4) | collective-permute-done | bytes 131104 | tf_op jit(solution)/shard_map/ppermute | solution.py:134
  54.8 0.3 collective-permute-start.6
  55.1 0.0 collective-permute-done.5.refs_6_
  55.1 2.4 %collective-permute-start.7 = (bf16[16,2048]{1,0:T(8,128)(2,1)S(1)}, bf16[16,2048]{1,0:T(8,128)(2,1)S(1)}, u32[]{:S(2)}, u32[]{:S(2)}) collective-permute-start(bf16[16,2048]{1,0:T(8,128)(2,1)S(1)} %slice.9), channel_id=1, source_target_pairs={{0,96},{32,0},{64,32},{96,64},{1,97},{33,1},{65,33},{97,65},{2,98}... | collective-permute-start | bytes 196616 | tf_op jit(solution)/shard_map/ppermute | solution.py:134
  57.6 0.7 stack.67.from_ref
  58.3 6.1 %collective-permute-start.8 = (bf16[32,2048]{1,0:T(8,128)(2,1)}, bf16[32,2048]{1,0:T(8,128)(2,1)S(1)}, u32[]{:S(2)}, u32[]{:S(2)}) collective-permute-start(bf16[32,2048]{1,0:T(8,128)(2,1)} %scale.1.refs_0_), channel_id=1, source_target_pairs={{0,16},{16,0},{1,17},{17,1},{2,18},{18,2},{3,19},{19,3},{4,20},{20... | collective-permute-start | bytes 393224 | tf_op jit(solution)/shard_map/ppermute | solution.py:130
  64.4 0.0 collective-permute-start.3
  64.4 0.0 collective-permute-done.2.refs_3_
  64.4 0.1 collective-permute-start.11
  64.5 0.0 collective-permute-done.6
  64.5 0.5 collective-permute-start.15
  65.0 0.0 collective-permute-done.7
  65.0 0.6 collective-permute-start.16
  65.6 0.7 pad_maximum_fusion.refs_7_
  66.3 0.0 collective-permute-done.8.refs_8_
  66.3 0.0 collective-permute-start.10
  66.3 0.0 collective-permute-done.11.refs_11_
  66.3 0.5 collective-permute-start.9
  66.8 2.7 %collective-permute-done.3.refs_4_ = bf16[32,2048]{1,0:T(8,128)(2,1)S(1)} collective-permute-done((bf16[32,2048]{1,0:T(8,128)(2,1)S(1)}, bf16[32,2048]{1,0:T(8,128)(2,1)S(1)}, u32[]{:S(2)}, u32[]{:S(2)}) %collective-permute-start.3) | collective-permute-done | bytes 131104 | tf_op jit(solution)/shard_map/ppermute | solution.py:130
  69.5 0.8 collective-permute-start.13
  70.3 0.0 collective-permute-done.15
  70.3 0.1 collective-permute-start.14
  70.4 0.0 collective-permute-done.16
  70.4 0.4 collective-permute-start.12
  70.8 0.7 pad_maximum_fusion.1.refs_15_
  71.5 0.0 collective-permute-done.10.refs_10_
  71.5 0.0 collective-permute-done.9.refs_9_
  71.5 0.0 collective-permute-done.13.refs_13_
  71.5 0.3 collective-permute-done.12.refs_12_
  71.9 0.0 collective-permute-done.14.refs_14_
  71.9 0.2 copy-done.8
  72.1 0.1 copy-done.9
  72.2 0.0 copy-done.10
  72.2 0.3 copy-done.12
  72.5 0.6 copy-done.11
  73.2 11.8 %scores.1 = f32[1,512,2048]{2,1,0:T(8,128)} custom-call(s32[16]{0:T(128)} %stack.67.from_ref, bf16[32,2048]{1,0:T(8,128)(2,1)} %scale.1.refs_0_, bf16[32,2048]{1,0:T(8,128)(2,1)} %copy-done.3, bf16[32,2048]{1,0:T(8,128)(2,1)} %copy-done.2, bf16[32,2048]{1,0:T(8,128)(2,1)} %copy-done.4, bf16[32,2048]{1,0:T(8,128)(2,1)} %copy-done.6, ...), custom_call_target="tpu_custom_call" | custom-call | tf_op jit(solution)/shard_map/scores/pallas_call | solution.py:190
  (23 shorter events, 0.0 us)
Async XLA Ops:
  44.5 5.2 %collective-permute-start.1 = (bf16[32,2048]{1,0:T(8,128)(2,1)}, bf16[32,2048]{1,0:T(8,128)(2,1)S(1)}, u32[]{:S(2)}, u32[]{:S(2)}) collective-permute-start(bf16[32,2048]{1,0:T(8,128)(2,1)} %scale.1.refs_0_), channel_id=1, source_target_pairs={{0,32},{32,64},{64,96},{96,0},{1,33},{33,65},{65,97},{97,1},{2,34}... | collective-permute-start | bytes 393224 | tf_op jit(solution)/shard_map/ppermute | solution.py:134
  44.5 5.2 %collective-permute-start = (bf16[32,2048]{1,0:T(8,128)(2,1)}, bf16[32,2048]{1,0:T(8,128)(2,1)S(1)}, u32[]{:S(2)}, u32[]{:S(2)}) collective-permute-start(bf16[32,2048]{1,0:T(8,128)(2,1)} %scale.1.refs_0_), channel_id=1, source_target_pairs={{0,128},{128,0},{1,129},{129,1},{2,130},{130,2},{3,131},{131,3},{4... | collective-permute-start | bytes 393224 | tf_op jit(solution)/shard_map/ppermute | solution.py:130
  49.8 22.1 %copy-start.2 = (bf16[32,2048]{1,0:T(8,128)(2,1)}, bf16[32,2048]{1,0:T(8,128)(2,1)S(1)}, u32[]{:S(2)}) copy-start(bf16[32,2048]{1,0:T(8,128)(2,1)S(1)} %collective-permute-done.1.refs_2_) | copy-start | bytes 393220
  49.8 5.0 %collective-permute-start.4 = (bf16[32,2048]{1,0:T(8,128)(2,1)S(1)}, bf16[32,2048]{1,0:T(8,128)(2,1)S(1)}, u32[]{:S(2)}, u32[]{:S(2)}) collective-permute-start(bf16[32,2048]{1,0:T(8,128)(2,1)S(1)} %collective-permute-done.1.refs_2_), channel_id=1, source_target_pairs={{0,32},{32,64},{64,96},{96,0},{1,33},{33,65},{65,97},{97,1},{2,34}... | collective-permute-start | bytes 393224 | tf_op jit(solution)/shard_map/ppermute | solution.py:134
  49.8 22.1 %copy-start.3 = (bf16[32,2048]{1,0:T(8,128)(2,1)}, bf16[32,2048]{1,0:T(8,128)(2,1)S(1)}, u32[]{:S(2)}) copy-start(bf16[32,2048]{1,0:T(8,128)(2,1)S(1)} %collective-permute-done.refs_1_) | copy-start | bytes 393220
  49.8 5.3 %collective-permute-start.5 = (bf16[32,2048]{1,0:T(8,128)(2,1)S(1)}, bf16[32,2048]{1,0:T(8,128)(2,1)S(1)}, u32[]{:S(2)}, u32[]{:S(2)}) collective-permute-start(bf16[32,2048]{1,0:T(8,128)(2,1)S(1)} %collective-permute-done.refs_1_), channel_id=1, source_target_pairs={{0,96},{32,0},{64,32},{96,64},{1,97},{33,1},{65,33},{97,65},{2,98}... | collective-permute-start | bytes 393224 | tf_op jit(solution)/shard_map/ppermute | solution.py:134
  52.4 12.0 %collective-permute-start.2 = (bf16[32,2048]{1,0:T(8,128)(2,1)}, bf16[32,2048]{1,0:T(8,128)(2,1)S(1)}, u32[]{:S(2)}, u32[]{:S(2)}) collective-permute-start(bf16[32,2048]{1,0:T(8,128)(2,1)} %scale.1.refs_0_), channel_id=1, source_target_pairs={{0,96},{32,0},{64,32},{96,64},{1,97},{33,1},{65,33},{97,65},{2,98}... | collective-permute-start | bytes 393224 | tf_op jit(solution)/shard_map/ppermute | solution.py:134
  54.8 17.1 %copy-start = (bf16[32,2048]{1,0:T(8,128)(2,1)}, bf16[32,2048]{1,0:T(8,128)(2,1)S(1)}, u32[]{:S(2)}) copy-start(bf16[32,2048]{1,0:T(8,128)(2,1)S(1)} %collective-permute-done.4.refs_5_) | copy-start | bytes 393220
  54.8 9.7 %collective-permute-start.6 = (bf16[16,2048]{1,0:T(8,128)(2,1)S(1)}, bf16[16,2048]{1,0:T(8,128)(2,1)S(1)}, u32[]{:S(2)}, u32[]{:S(2)}) collective-permute-start(bf16[16,2048]{1,0:T(8,128)(2,1)S(1)} %slice.8), channel_id=1, source_target_pairs={{0,128},{128,0},{1,129},{129,1},{2,130},{130,2},{3,131},{131,3},{4... | collective-permute-start | bytes 196616 | tf_op jit(solution)/shard_map/ppermute | solution.py:130
  55.1 16.8 %copy-start.1 = (bf16[32,2048]{1,0:T(8,128)(2,1)}, bf16[32,2048]{1,0:T(8,128)(2,1)S(1)}, u32[]{:S(2)}) copy-start(bf16[32,2048]{1,0:T(8,128)(2,1)S(1)} %collective-permute-done.5.refs_6_) | copy-start | bytes 393220
  55.1 9.9 %collective-permute-start.7 = (bf16[16,2048]{1,0:T(8,128)(2,1)S(1)}, bf16[16,2048]{1,0:T(8,128)(2,1)S(1)}, u32[]{:S(2)}, u32[]{:S(2)}) collective-permute-start(bf16[16,2048]{1,0:T(8,128)(2,1)S(1)} %slice.9), channel_id=1, source_target_pairs={{0,96},{32,0},{64,32},{96,64},{1,97},{33,1},{65,33},{97,65},{2,98}... | collective-permute-start | bytes 196616 | tf_op jit(solution)/shard_map/ppermute | solution.py:134
  58.3 8.0 %collective-permute-start.8 = (bf16[32,2048]{1,0:T(8,128)(2,1)}, bf16[32,2048]{1,0:T(8,128)(2,1)S(1)}, u32[]{:S(2)}, u32[]{:S(2)}) collective-permute-start(bf16[32,2048]{1,0:T(8,128)(2,1)} %scale.1.refs_0_), channel_id=1, source_target_pairs={{0,16},{16,0},{1,17},{17,1},{2,18},{18,2},{3,19},{19,3},{4,20},{20... | collective-permute-start | bytes 393224 | tf_op jit(solution)/shard_map/ppermute | solution.py:130
  64.4 5.1 %collective-permute-start.3 = (bf16[32,2048]{1,0:T(8,128)(2,1)S(1)}, bf16[32,2048]{1,0:T(8,128)(2,1)S(1)}, u32[]{:S(2)}, u32[]{:S(2)}) collective-permute-start(bf16[32,2048]{1,0:T(8,128)(2,1)S(1)} %collective-permute-done.1.refs_2_), channel_id=1, source_target_pairs={{0,128},{128,0},{1,129},{129,1},{2,130},{130,2},{3,131},{131,3},{4... | collective-permute-start | bytes 393224 | tf_op jit(solution)/shard_map/ppermute | solution.py:130
  64.4 7.5 %copy-start.4 = (bf16[32,2048]{1,0:T(8,128)(2,1)}, bf16[32,2048]{1,0:T(8,128)(2,1)S(1)}, u32[]{:S(2)}) copy-start(bf16[32,2048]{1,0:T(8,128)(2,1)S(1)} %collective-permute-done.2.refs_3_) | copy-start | bytes 393220
  64.4 1.9 %collective-permute-start.11 = (bf16[32,2048]{1,0:T(8,128)(2,1)S(1)}, bf16[32,2048]{1,0:T(8,128)(2,1)S(1)}, u32[]{:S(2)}, u32[]{:S(2)}) collective-permute-start(bf16[32,2048]{1,0:T(8,128)(2,1)S(1)} %collective-permute-done.2.refs_3_), channel_id=1, source_target_pairs={{0,16},{16,0},{1,17},{17,1},{2,18},{18,2},{3,19},{19,3},{4,20},{20... | collective-permute-start | bytes 393224 | tf_op jit(solution)/shard_map/ppermute | solution.py:130
  64.5 5.8 %collective-permute-start.15 = (bf16[16,2048]{1,0:T(8,128)(2,1)S(1)}, bf16[16,2048]{1,0:T(8,128)(2,1)S(1)}, u32[]{:S(2)}, u32[]{:S(2)}) collective-permute-start(bf16[16,2048]{1,0:T(8,128)(2,1)S(1)} %collective-permute-done.6), channel_id=1, source_target_pairs={{0,16},{16,0},{1,17},{17,1},{2,18},{18,2},{3,19},{19,3},{4,20},{20... | collective-permute-start | bytes 196616 | tf_op jit(solution)/shard_map/ppermute | solution.py:130
  65.0 5.4 %collective-permute-start.16 = (bf16[16,2048]{1,0:T(8,128)(2,1)S(1)}, bf16[16,2048]{1,0:T(8,128)(2,1)S(1)}, u32[]{:S(2)}, u32[]{:S(2)}) collective-permute-start(bf16[16,2048]{1,0:T(8,128)(2,1)S(1)} %collective-permute-done.7), channel_id=1, source_target_pairs={{0,16},{16,0},{1,17},{17,1},{2,18},{18,2},{3,19},{19,3},{4,20},{20... | collective-permute-start | bytes 196616 | tf_op jit(solution)/shard_map/ppermute | solution.py:130
  66.3 5.6 %copy-start.5 = (bf16[32,2048]{1,0:T(8,128)(2,1)}, bf16[32,2048]{1,0:T(8,128)(2,1)S(1)}, u32[]{:S(2)}) copy-start(bf16[32,2048]{1,0:T(8,128)(2,1)S(1)} %collective-permute-done.8.refs_8_) | copy-start | bytes 393220
  66.3 5.2 %collective-permute-start.10 = (bf16[32,2048]{1,0:T(8,128)(2,1)S(1)}, bf16[32,2048]{1,0:T(8,128)(2,1)S(1)}, u32[]{:S(2)}, u32[]{:S(2)}) collective-permute-start(bf16[32,2048]{1,0:T(8,128)(2,1)S(1)} %collective-permute-done.1.refs_2_), channel_id=1, source_target_pairs={{0,16},{16,0},{1,17},{17,1},{2,18},{18,2},{3,19},{19,3},{4,20},{20... | collective-permute-start | bytes 393224 | tf_op jit(solution)/shard_map/ppermute | solution.py:130
  66.3 5.6 %copy-start.7 = (bf16[32,2048]{1,0:T(8,128)(2,1)}, bf16[32,2048]{1,0:T(8,128)(2,1)S(1)}, u32[]{:S(2)}) copy-start(bf16[32,2048]{1,0:T(8,128)(2,1)S(1)} %collective-permute-done.11.refs_11_) | copy-start | bytes 393220
  66.3 5.2 %collective-permute-start.9 = (bf16[32,2048]{1,0:T(8,128)(2,1)S(1)}, bf16[32,2048]{1,0:T(8,128)(2,1)S(1)}, u32[]{:S(2)}, u32[]{:S(2)}) collective-permute-start(bf16[32,2048]{1,0:T(8,128)(2,1)S(1)} %collective-permute-done.refs_1_), channel_id=1, source_target_pairs={{0,16},{16,0},{1,17},{17,1},{2,18},{18,2},{3,19},{19,3},{4,20},{20... | collective-permute-start | bytes 393224 | tf_op jit(solution)/shard_map/ppermute | solution.py:130
  69.5 2.4 %copy-start.6 = (bf16[32,2048]{1,0:T(8,128)(2,1)}, bf16[32,2048]{1,0:T(8,128)(2,1)S(1)}, u32[]{:S(2)}) copy-start(bf16[32,2048]{1,0:T(8,128)(2,1)S(1)} %collective-permute-done.3.refs_4_) | copy-start | bytes 393220
  69.5 2.0 %collective-permute-start.13 = (bf16[32,2048]{1,0:T(8,128)(2,1)S(1)}, bf16[32,2048]{1,0:T(8,128)(2,1)S(1)}, u32[]{:S(2)}, u32[]{:S(2)}) collective-permute-start(bf16[32,2048]{1,0:T(8,128)(2,1)S(1)} %collective-permute-done.4.refs_5_), channel_id=1, source_target_pairs={{0,16},{16,0},{1,17},{17,1},{2,18},{18,2},{3,19},{19,3},{4,20},{20... | collective-permute-start | bytes 393224 | tf_op jit(solution)/shard_map/ppermute | solution.py:130
  70.3 1.5 %collective-permute-start.14 = (bf16[32,2048]{1,0:T(8,128)(2,1)S(1)}, bf16[32,2048]{1,0:T(8,128)(2,1)S(1)}, u32[]{:S(2)}, u32[]{:S(2)}) collective-permute-start(bf16[32,2048]{1,0:T(8,128)(2,1)S(1)} %collective-permute-done.5.refs_6_), channel_id=1, source_target_pairs={{0,16},{16,0},{1,17},{17,1},{2,18},{18,2},{3,19},{19,3},{4,20},{20... | collective-permute-start | bytes 393224 | tf_op jit(solution)/shard_map/ppermute | solution.py:130
  70.4 1.4 %collective-permute-start.12 = (bf16[32,2048]{1,0:T(8,128)(2,1)S(1)}, bf16[32,2048]{1,0:T(8,128)(2,1)S(1)}, u32[]{:S(2)}, u32[]{:S(2)}) collective-permute-start(bf16[32,2048]{1,0:T(8,128)(2,1)S(1)} %collective-permute-done.3.refs_4_), channel_id=1, source_target_pairs={{0,16},{16,0},{1,17},{17,1},{2,18},{18,2},{3,19},{19,3},{4,20},{20... | collective-permute-start | bytes 393224 | tf_op jit(solution)/shard_map/ppermute | solution.py:130
  71.5 0.6 copy-start.8
  71.5 0.7 copy-start.9
  71.5 0.7 copy-start.10
  71.8 0.7 copy-start.12
  72.5 0.6 copy-start.11

commit v2 on v1

--- a/solution.py
+++ b/solution.py
@@ -25,11 +25,23 @@
 VM = pl.BlockSpec(memory_space=pltpu.VMEM)
 
 
+def room(mib):
+    return pltpu.CompilerParams(vmem_limit_bytes=mib << 20)
+
+
 def iota(shape, axis):
     return lax.broadcasted_iota(jnp.int32, shape, axis)
 
 
-def slot_kernel(act_ref, grad_ref, ids_ref, own_ref, send_ref):
+def slot_kernel(act_hbm, grad_hbm, ids_hbm, own_hbm, po_hbm, pi_hbm, train_hbm, send_ref, po_ref, pi_ref, train_ref,
+                act_ref, grad_ref, ids_ref, own_ref, sem):
+    sources = (ids_hbm, own_hbm, act_hbm, grad_hbm, po_hbm, pi_hbm, train_hbm)
+    targets = (ids_ref, own_ref, act_ref, grad_ref, po_ref, pi_ref, train_ref)
+    copies = [pltpu.make_async_copy(a, b, sem.at[i]) for i, (a, b) in enumerate(zip(sources, targets))]
+    for copy in copies:
+        copy.start()
+    copies[0].wait()
+    copies[1].wait()
     ids = ids_ref[...]
     ids_col = jnp.transpose(jnp.broadcast_to(ids, (8, TOK)))[:, :1]
     own_col = jnp.transpose(jnp.broadcast_to(own_ref[...], (8, DOCS)))[:, :1]
@@ -48,6 +60,8 @@
     group = slot // 256
     inner = slot % 256
     hot = (iota((256, TOK), 0) == inner).astype(F32).astype(BF)
+    copies[2].wait()
+    copies[3].wait()
     rows = jnp.concatenate([act_ref[0], grad_ref[0]], axis=0)
     zero = jnp.zeros_like(rows)
     for o in range(BLK // 2):
@@ -55,6 +69,8 @@
         got = lax.dot_general(part, hot, NT, preferred_element_type=F32).astype(BF)
         send_ref[2 * o] = got[:, :LANES]
         send_ref[2 * o + 1] = got[:, LANES:]
+    for copy in copies[4:]:
+        copy.wait()
 
 
 def split(x):
@@ -114,16 +130,27 @@
     doc_ref[...] = (cond_ref[...] * inverse).astype(BF)
 
 
-def score_kernel(count, from_ref, *refs):
-    blocks, train_ref, out_ref, docs_ref = refs[:count], refs[count], refs[count + 1], refs[count + 2]
-
-    @pl.when(pl.program_id(0) == 0)
-    def _():
-        for i in range(count):
-            at = pl.multiple_of(from_ref[i] * OWN, OWN)
-            docs_ref[pl.ds(at, OWN), :] = blocks[i][...]
-
-    out_ref[0] = lax.dot_general(docs_ref[...], train_ref[0], NT, preferred_element_type=F32)
+def score_kernel(places, *refs):
+    count = len(places)
+    blocks, train_ref, out_hbm, buffer, sem = refs[:count], refs[count], *refs[-3:]
+    x, y, c = (lax.axis_index(a) for a in BLK_AXES)
+    docs = jnp.concatenate([b[...] for b in blocks], axis=0)
+    tile = 512
+    copies = []
+    for i in range(buffer.shape[1] // tile):
+        cols = pl.ds(i * tile, tile)
+        buffer[:, cols] = lax.dot_general(docs, train_ref[0, cols, :], NT, preferred_element_type=F32)
+        for j, (dx, dy, dc) in enumerate(places):
+            at = (((x ^ dx) * 4 + (y + dy) % 4) * 2 + (c ^ dc)) * OWN
+            copy = pltpu.make_async_copy(
+                buffer.at[pl.ds(j * OWN, OWN), cols],
+                out_hbm.at[0, pl.ds(pl.multiple_of(at, OWN), OWN), cols],
+                sem.at[i, j],
+            )
+            copy.start()
+            copies.append(copy)
+    for copy in copies:
+        copy.wait()
 
 
 def swap(x, axis):
@@ -134,37 +161,53 @@
     return lax.ppermute(x, "y", [(i, (i + by) % 4) for i in range(4)])
 
 
-def gather_docs(doc):
-    x, y, c = (lax.axis_index(a) for a in BLK_AXES)
-
-    def source(dx, dy, dc):
-        return ((x ^ dx) * 4 + (y + dy) % 4) * 2 + (c ^ dc)
-
-    half = OWN // 2
-    got = {(0, 0): doc}
-    got[1, 0] = swap(doc, "xl")
-    got[0, 3] = turn(doc, 1)
-    got[0, 1] = turn(doc, -1)
-    got[1, 3] = swap(got[0, 3], "xl")
-    got[0, 2] = turn(got[0, 3], 1)
-    got[1, 1] = turn(got[1, 0], -1)
-    last = [swap(got[0, 2][:half], "xl"), turn(got[1, 1][half:], -1)]
-    mates = {k: swap(v, "core") for k, v in got.items()}
-    got[1, 2] = jnp.concatenate(last, axis=0)
-    mates[1, 2] = jnp.concatenate([swap(v, "core") for v in last], axis=0)
-    blocks = [*got.values(), *mates.values()]
-    places = [source(*k, 0) for k in got] + [source(*k, 1) for k in mates]
-    return blocks, jnp.stack(places).astype(jnp.int32)
+def score(name, places, blocks, train, out=None):
+    rows = train.shape[1]
+    hbm = pl.BlockSpec(memory_space=pltpu.HBM)
+    more = () if out is None else (out,)
+    return pl.pallas_call(
+        functools.partial(score_kernel, places),
+        out_shape=pltpu.HBM((1, DOCS, rows), F32),
+        in_specs=[VM] * (len(blocks) + 1) + [hbm] * len(more),
+        out_specs=hbm,
+        scratch_shapes=[
+            pltpu.VMEM((len(blocks) * OWN, rows), F32),
+            pltpu.SemaphoreType.DMA((rows // 512, len(blocks))),
+        ],
+        input_output_aliases={len(blocks) + 1: 0} if more else {},
+        name=name,
+        compiler_params=room(8),
+    )(*blocks, train, *more)
+
+
+def pair(block):
+    return [block, swap(block, "core")]
+
+
+def label(*offsets):
+    return [(dx, dy, dc) for dx, dy in offsets for dc in (0, 1)]
 
 
 def body(act, grad, train, pre_out, pre_in, doc_ids, owners):
-    send = pl.pallas_call(
+    hbm = pl.BlockSpec(memory_space=pltpu.HBM)
+    ids, own = doc_ids.reshape(1, TOK), owners.reshape(1, DOCS)
+    kept = (pre_out, pre_in, train)
+    loaded = (act, grad, ids, own)
+    send, pre_out, pre_in, train = pl.pallas_call(
         slot_kernel,
-        out_shape=jax.ShapeDtypeStruct((BLK, W, LANES), BF),
-        in_specs=[VM] * 4,
-        out_specs=VM,
+        out_shape=(
+            jax.ShapeDtypeStruct((BLK, W, LANES), BF),
+            *(pltpu.VMEM(v.shape, v.dtype) for v in kept),
+        ),
+        in_specs=[hbm] * 7,
+        out_specs=[VM] * 4,
+        scratch_shapes=[
+            *(pltpu.VMEM(v.shape, v.dtype) for v in loaded),
+            pltpu.SemaphoreType.DMA((7,)),
+        ],
         name="slots",
-    )(act, grad, doc_ids.reshape(1, TOK), owners.reshape(1, DOCS))
+        compiler_params=room(24),
+    )(*(pltpu.with_memory_space_constraint(v, pltpu.HBM) for v in (*loaded, *kept)))
     received = lax.all_to_all(send, BLK_AXES, split_axis=0, concat_axis=0, tiled=True)
     cond, squares = pl.pallas_call(
         cond_kernel,
@@ -175,6 +218,7 @@
         in_specs=[VM] * 3,
         out_specs=(VM, VM),
         name="condition",
+        compiler_params=room(16),
     )(received, pre_out, pre_in)
     squares = lax.all_to_all(squares, MOD_AXES, split_axis=0, concat_axis=0, tiled=True)
     doc = pl.pallas_call(
@@ -183,22 +227,16 @@
         in_specs=[VM] * 2,
         out_specs=VM,
         name="scale",
+        compiler_params=room(2),
     )(cond, squares)
-    blocks, places = gather_docs(doc)
-    tile = 256
-    rows = train.shape[1]
-    return pl.pallas_call(
-        functools.partial(score_kernel, len(blocks)),
-        out_shape=jax.ShapeDtypeStruct((1, DOCS, rows), F32),
-        grid_spec=pltpu.PrefetchScalarGridSpec(
-            num_scalar_prefetch=1,
-            grid=(rows // tile,),
-            in_specs=[VM] * len(blocks) + [pl.BlockSpec((1, tile, F), lambda i, s: (0, i, 0))],
-            out_specs=pl.BlockSpec((1, DOCS, tile), lambda i, s: (0, 0, i)),
-            scratch_shapes=[pltpu.VMEM((DOCS, F), BF)],
-        ),
-        name="scores",
-    )(places, *blocks, train)
+    side, above, below, over = swap(doc, "xl"), turn(doc, 1), turn(doc, -1), turn(doc, 2)
+    near = pair(doc) + pair(side) + pair(above) + pair(below)
+    side_above, side_below, side_over = swap(above, "xl"), turn(side, -1), swap(over, "xl")
+    out = score("near", label((0, 0), (1, 0), (0, 3), (0, 1)), near, train)
+    far = lax.optimization_barrier((over, side_above, side_below, side_over, out))
+    over, side_above, side_below, side_over, out = far
+    far = pair(over) + pair(side_above) + pair(side_below) + pair(side_over)
+    return score("far", label((0, 2), (1, 3), (1, 1), (1, 2)), far, train, out)
 
 
 def solution(mesh):

time: 85.4 us -> 67.9 us (0.80)
  Pallas kernels: 21.4 us -> 13.1 us
  waiting for transfers between devices: 10.1 us -> 4.29 us
  local copies, waits for them, and re-layouts: 1.97 us -> 0 us
  other arithmetic: 1.33 us -> 0 us
    ppermute x5 -> x4, waiting for transfers between devices: 7.08 us -> 0.01 us  [turn(): return lax.ppermute(x, 'y', [(i, (i + by) % 4) for i in range(4)])]
    pallas_call x2 -> x3, Pallas kernels: 15.5 us -> 10.5 us  [the longest x2 6.85 us: score(): pl.pallas_call(functools.partial(score_kernel, places), out_shape=pltpu.H...]
    ppermute x12 -> x11, starting transfers between devices: 9.86 us -> 13 us  [swap(): return lax.ppermute(x, axis, [(0, 1), (1, 0)])]
    ppermute x5 -> x4, starting transfers between devices: 5.19 us -> 2.85 us  [turn(): return lax.ppermute(x, 'y', [(i, (i + by) % 4) for i in range(4)])]
    pallas_call x1, Pallas kernels: 4.1 us -> 2.46 us  [body(): pl.pallas_call(cond_kernel, out_shape=(jax.ShapeDtypeStruct((OWN, F), F32...]
    pallas_call x1, Pallas kernels: 1.79 us -> 0.18 us  [body(): pl.pallas_call(scale_kernel, out_shape=jax.ShapeDtypeStruct((OWN, F), BF)...]
    concatenate x2 -> x0, other arithmetic: 1.33 us -> none  [the longest x1 0.67 us: gather_docs(): got[1, 2] = jnp.concatenate(last, axis=0)]
    unnamed x26 -> x0, local copies, waits for them, and re-layouts: 1.27 us -> none
  transfers between devices with their start and end apart: 17 -> 15, of which waited for: 4 -> 6; matrix products, arithmetic and copies ran while one was open for 2% -> 0% of each run, Pallas kernels for 0% -> 5%
where the time goes in v2:
time: 67.9 us; the launch traced here: 67.7 us
  blocking collectives  34.2 us (50%)
  starting transfers between devices  15.8 us (23%)
  Pallas kernels  13.1 us (19%)
  waiting for transfers between devices  4.29 us (6%)
    all_to_all x1, blocking collectives, body(): lax.all_to_all(squares, MOD_AXES, split_axis=0, concat_axis=0, tiled=True)  19.1 us
    all_to_all x1, blocking collectives, body(): lax.all_to_all(send, BLK_AXES, split_axis=0, concat_axis=0, tiled=True)  15.1 us
    ppermute x11, starting transfers between devices, swap(): return lax.ppermute(x, axis, [(0, 1), (1, 0)])  13 us
    pallas_call x2, Pallas kernels, score(): pl.pallas_call(functools.partial(score_kernel, places), out_shape=pltpu.H...  6.85 us
    ppermute x11, waiting for transfers between devices, swap(): return lax.ppermute(x, axis, [(0, 1), (1, 0)])  4.28 us
    pallas_call x1, Pallas kernels, body(): pl.pallas_call(slot_kernel, out_shape=(jax.ShapeDtypeStruct((BLK, W, LANE...  3.63 us
    ppermute x4, starting transfers between devices, turn(): return lax.ppermute(x, 'y', [(i, (i + by) % 4) for i in range(4)])  2.85 us
    pallas_call x1, Pallas kernels, body(): pl.pallas_call(cond_kernel, out_shape=(jax.ShapeDtypeStruct((OWN, F), F32...  2.46 us
  transfers between devices with their start and end apart: 15, of which 6 were waited for; matrix products, arithmetic and copies ran while one was open for 0% of the time, Pallas kernels for 5%

profile of v2, /device:TPU:1, one launch (start us, length us, event | category | flops | bytes accessed | tf_op | source)
XLA Modules:
  0.0 67.7 jit_solution(4161483041092356927)
XLA Ops:
  0.0 3.6 %slots.1 = (bf16[16,96,128]{2,1,0:T(8,128)(2,1)S(1)}, f32[1,64,64]{2,1,0:T(8,128)S(1)}, f32[1,32,32]{2,1,0:T(8,128)S(1)}, bf16[1,2048,2048]{2,1,0:T(8,128)(2,1)S(1)}) custom-call(bf16[1,32,1024]{2,1,0:T(8,128)(2,1)} %act_hbm.1, bf16[1,64,1024]{2,1,0:T(8,128)(2,1)} %grad_hbm.1, s32[1,1024]{1,0:T(1,128)} %bitcast.2, s32[1,512]{1,0:T(1,128)} %bitcast.3, ...), custom_call_target="tpu_custom_call" | custom-call | tf_op jit(solution)/shard_map/slots/pallas_call | solution.py:196
  3.6 15.1 %all_to_all.10.recv_ref = bf16[16,96,128]{2,1,0:T(8,128)(2,1)S(1)} all-to-all(bf16[16,96,128]{2,1,0:T(8,128)(2,1)S(1)} %get-tuple-element.16), channel_id=1, replica_groups=mesh['xl'=2,'y'=4,'core'=2,'xh'=2,'z'=8] {'xl','y','core'}, dimensions={0} | all-to-all | bytes 786432 | tf_op jit(solution)/shard_map/all_to_all | solution.py:211
  18.7 2.5 %condition.1 = (f32[32,2048]{1,0:T(8,128)S(1)}, f32[16,8,128]{2,1,0:T(8,128)S(1)}) custom-call(bf16[16,96,128]{2,1,0:T(8,128)(2,1)S(1)} %all_to_all.10.recv_ref, f32[1,64,64]{2,1,0:T(8,128)S(1)} %get-tuple-element.17.po_ref, f32[1,32,32]{2,1,0:T(8,128)S(1)} %get-tuple-element.18.pi_ref), custom_call_target="tpu_custom_call" | custom-call | tf_op jit(solution)/shard_map/condition/pallas_call | solution.py:212
  21.2 19.1 %all_to_all.11.squares_ref = f32[16,8,128]{2,1,0:T(8,128)S(1)} all-to-all(f32[16,8,128]{2,1,0:T(8,128)S(1)} %get-tuple-element.20), channel_id=1, replica_groups=mesh['xl'=2,'y'=4,'core'=2,'xh'=2,'z'=8] {'xh','z'}, dimensions={0} | all-to-all | bytes 131072 | tf_op jit(solution)/shard_map/all_to_all | solution.py:223
  40.3 0.2 scale.1.refs_0_
  40.5 1.7 %collective-permute-start.9 = (bf16[32,2048]{1,0:T(8,128)(2,1)S(1)}, bf16[32,2048]{1,0:T(8,128)(2,1)S(1)}, u32[]{:S(2)}, u32[]{:S(2)}) collective-permute-start(bf16[32,2048]{1,0:T(8,128)(2,1)S(1)} %scale.1.refs_0_), channel_id=1, source_target_pairs={{0,96},{32,0},{64,32},{96,64},{1,97},{33,1},{65,33},{97,65},{2,98}... | collective-permute-start | bytes 393224 | tf_op jit(solution)/shard_map/ppermute | solution.py:161
  42.2 0.0 collective-permute-start.3
  42.2 0.0 collective-permute-start.1
  42.3 2.9 %collective-permute-start.6 = (bf16[32,2048]{1,0:T(8,128)(2,1)S(1)}, bf16[32,2048]{1,0:T(8,128)(2,1)S(1)}, u32[]{:S(2)}, u32[]{:S(2)}) collective-permute-start(bf16[32,2048]{1,0:T(8,128)(2,1)S(1)} %scale.1.refs_0_), channel_id=1, source_target_pairs={{0,16},{16,0},{1,17},{17,1},{2,18},{18,2},{3,19},{19,3},{4,20},{20... | collective-permute-start | bytes 393224 | tf_op jit(solution)/shard_map/ppermute | solution.py:157
  45.2 1.1 %collective-permute-start = (bf16[32,2048]{1,0:T(8,128)(2,1)S(1)}, bf16[32,2048]{1,0:T(8,128)(2,1)S(1)}, u32[]{:S(2)}, u32[]{:S(2)}) collective-permute-start(bf16[32,2048]{1,0:T(8,128)(2,1)S(1)} %scale.1.refs_0_), channel_id=1, source_target_pairs={{0,64},{32,96},{64,0},{96,32},{1,65},{33,97},{65,1},{97,33},{2,66}... | collective-permute-start | bytes 393224 | tf_op jit(solution)/shard_map/ppermute | solution.py:161
  46.3 0.0 collective-permute-done.9.refs_6_
  46.3 1.9 %collective-permute-start.10 = (bf16[32,2048]{1,0:T(8,128)(2,1)S(1)}, bf16[32,2048]{1,0:T(8,128)(2,1)S(1)}, u32[]{:S(2)}, u32[]{:S(2)}) collective-permute-start(bf16[32,2048]{1,0:T(8,128)(2,1)S(1)} %collective-permute-done.9.refs_6_), channel_id=1, source_target_pairs={{0,16},{16,0},{1,17},{17,1},{2,18},{18,2},{3,19},{19,3},{4,20},{20... | collective-permute-start | bytes 393224 | tf_op jit(solution)/shard_map/ppermute | solution.py:157
  48.1 0.0 collective-permute-done.3.refs_2_
  48.2 1.0 %collective-permute-start.7 = (bf16[32,2048]{1,0:T(8,128)(2,1)S(1)}, bf16[32,2048]{1,0:T(8,128)(2,1)S(1)}, u32[]{:S(2)}, u32[]{:S(2)}) collective-permute-start(bf16[32,2048]{1,0:T(8,128)(2,1)S(1)} %collective-permute-done.3.refs_2_), channel_id=1, source_target_pairs={{0,16},{16,0},{1,17},{17,1},{2,18},{18,2},{3,19},{19,3},{4,20},{20... | collective-permute-start | bytes 393224 | tf_op jit(solution)/shard_map/ppermute | solution.py:157
  49.1 0.0 collective-permute-done.1.refs_4_
  49.1 4.0 %collective-permute-start.8 = (bf16[32,2048]{1,0:T(8,128)(2,1)S(1)}, bf16[32,2048]{1,0:T(8,128)(2,1)S(1)}, u32[]{:S(2)}, u32[]{:S(2)}) collective-permute-start(bf16[32,2048]{1,0:T(8,128)(2,1)S(1)} %collective-permute-done.1.refs_4_), channel_id=1, source_target_pairs={{0,16},{16,0},{1,17},{17,1},{2,18},{18,2},{3,19},{19,3},{4,20},{20... | collective-permute-start | bytes 393224 | tf_op jit(solution)/shard_map/ppermute | solution.py:157
  53.2 0.0 collective-permute-done.6.refs_1_
  53.2 0.0 collective-permute-start.4
  53.2 0.0 collective-permute-done.refs_0_
  53.2 1.8 %collective-permute-start.2 = (bf16[32,2048]{1,0:T(8,128)(2,1)S(1)}, bf16[32,2048]{1,0:T(8,128)(2,1)S(1)}, u32[]{:S(2)}, u32[]{:S(2)}) collective-permute-start(bf16[32,2048]{1,0:T(8,128)(2,1)S(1)} %collective-permute-done.1.refs_4_), channel_id=1, source_target_pairs={{0,128},{128,0},{1,129},{129,1},{2,130},{130,2},{3,131},{131,3},{4... | collective-permute-start | bytes 393224 | tf_op jit(solution)/shard_map/ppermute | solution.py:157
  55.0 0.0 collective-permute-done.10.refs_7_
  55.0 0.3 collective-permute-start.5
  55.3 0.0 collective-permute-done.7.refs_3_
  55.3 0.0 collective-permute-done.8.refs_5_
  55.3 3.4 %near.1.refs_9_ = f32[1,512,2048]{2,1,0:T(8,128)} custom-call(bf16[32,2048]{1,0:T(8,128)(2,1)S(1)} %scale.1.refs_0_, bf16[32,2048]{1,0:T(8,128)(2,1)S(1)} %collective-permute-done.6.refs_1_, bf16[32,2048]{1,0:T(8,128)(2,1)S(1)} %collective-permute-done.3.refs_2_, bf16[32,2048]{1,0:T(8,128)(2,1)S(1)} %collective-permute-done.7.refs_3_, ...), custom_call_target="tpu_custom_call" | custom-call | tf_op jit(solution)/shard_map/near/pallas_call | solution.py:168
  58.7 0.0 collective-permute-done.4.refs_4_
  58.7 0.1 collective-permute-done.2.refs_2_
  58.9 2.8 %collective-permute-done.5.refs_6_ = bf16[32,2048]{1,0:T(8,128)(2,1)S(1)} collective-permute-done((bf16[32,2048]{1,0:T(8,128)(2,1)S(1)}, bf16[32,2048]{1,0:T(8,128)(2,1)S(1)}, u32[]{:S(2)}, u32[]{:S(2)}) %collective-permute-start.5) | collective-permute-done | bytes 131104 | tf_op jit(solution)/shard_map/ppermute | solution.py:157
  61.7 0.6 collective-permute-start.11
  62.3 0.0 collective-permute-start.12
  62.3 0.5 collective-permute-start.13
  62.8 0.0 collective-permute-start.14
  62.8 0.5 collective-permute-done.11.refs_1_
  63.2 0.4 collective-permute-done.12.refs_3_
  63.6 0.2 collective-permute-done.13.refs_5_
  63.8 0.3 collective-permute-done.14.refs_7_
  64.1 3.4 %far.1 = f32[1,512,2048]{2,1,0:T(8,128)} custom-call(bf16[32,2048]{1,0:T(8,128)(2,1)S(1)} %collective-permute-done.refs_0_, bf16[32,2048]{1,0:T(8,128)(2,1)S(1)} %collective-permute-done.11.refs_1_, bf16[32,2048]{1,0:T(8,128)(2,1)S(1)} %collective-permute-done.2.refs_2_, ...), custom_call_target="tpu_custom_call", output_to_operand_aliasing={{}: (9, {})} | custom-call | tf_op jit(solution)/shard_map/far/pallas_call | solution.py:168
Async XLA Ops:
  40.5 5.8 %collective-permute-start.9 = (bf16[32,2048]{1,0:T(8,128)(2,1)S(1)}, bf16[32,2048]{1,0:T(8,128)(2,1)S(1)}, u32[]{:S(2)}, u32[]{:S(2)}) collective-permute-start(bf16[32,2048]{1,0:T(8,128)(2,1)S(1)} %scale.1.refs_0_), channel_id=1, source_target_pairs={{0,96},{32,0},{64,32},{96,64},{1,97},{33,1},{65,33},{97,65},{2,98}... | collective-permute-start | bytes 393224 | tf_op jit(solution)/shard_map/ppermute | solution.py:161
  42.2 5.9 %collective-permute-start.3 = (bf16[32,2048]{1,0:T(8,128)(2,1)S(1)}, bf16[32,2048]{1,0:T(8,128)(2,1)S(1)}, u32[]{:S(2)}, u32[]{:S(2)}) collective-permute-start(bf16[32,2048]{1,0:T(8,128)(2,1)S(1)} %scale.1.refs_0_), channel_id=1, source_target_pairs={{0,128},{128,0},{1,129},{129,1},{2,130},{130,2},{3,131},{131,3},{4... | collective-permute-start | bytes 393224 | tf_op jit(solution)/shard_map/ppermute | solution.py:157
  42.2 6.9 %collective-permute-start.1 = (bf16[32,2048]{1,0:T(8,128)(2,1)S(1)}, bf16[32,2048]{1,0:T(8,128)(2,1)S(1)}, u32[]{:S(2)}, u32[]{:S(2)}) collective-permute-start(bf16[32,2048]{1,0:T(8,128)(2,1)S(1)} %scale.1.refs_0_), channel_id=1, source_target_pairs={{0,32},{32,64},{64,96},{96,0},{1,33},{33,65},{65,97},{97,1},{2,34}... | collective-permute-start | bytes 393224 | tf_op jit(solution)/shard_map/ppermute | solution.py:161
  42.3 10.9 %collective-permute-start.6 = (bf16[32,2048]{1,0:T(8,128)(2,1)S(1)}, bf16[32,2048]{1,0:T(8,128)(2,1)S(1)}, u32[]{:S(2)}, u32[]{:S(2)}) collective-permute-start(bf16[32,2048]{1,0:T(8,128)(2,1)S(1)} %scale.1.refs_0_), channel_id=1, source_target_pairs={{0,16},{16,0},{1,17},{17,1},{2,18},{18,2},{3,19},{19,3},{4,20},{20... | collective-permute-start | bytes 393224 | tf_op jit(solution)/shard_map/ppermute | solution.py:157
  45.2 8.0 %collective-permute-start = (bf16[32,2048]{1,0:T(8,128)(2,1)S(1)}, bf16[32,2048]{1,0:T(8,128)(2,1)S(1)}, u32[]{:S(2)}, u32[]{:S(2)}) collective-permute-start(bf16[32,2048]{1,0:T(8,128)(2,1)S(1)} %scale.1.refs_0_), channel_id=1, source_target_pairs={{0,64},{32,96},{64,0},{96,32},{1,65},{33,97},{65,1},{97,33},{2,66}... | collective-permute-start | bytes 393224 | tf_op jit(solution)/shard_map/ppermute | solution.py:161
  46.3 8.7 %collective-permute-start.10 = (bf16[32,2048]{1,0:T(8,128)(2,1)S(1)}, bf16[32,2048]{1,0:T(8,128)(2,1)S(1)}, u32[]{:S(2)}, u32[]{:S(2)}) collective-permute-start(bf16[32,2048]{1,0:T(8,128)(2,1)S(1)} %collective-permute-done.9.refs_6_), channel_id=1, source_target_pairs={{0,16},{16,0},{1,17},{17,1},{2,18},{18,2},{3,19},{19,3},{4,20},{20... | collective-permute-start | bytes 393224 | tf_op jit(solution)/shard_map/ppermute | solution.py:157
  48.2 7.1 %collective-permute-start.7 = (bf16[32,2048]{1,0:T(8,128)(2,1)S(1)}, bf16[32,2048]{1,0:T(8,128)(2,1)S(1)}, u32[]{:S(2)}, u32[]{:S(2)}) collective-permute-start(bf16[32,2048]{1,0:T(8,128)(2,1)S(1)} %collective-permute-done.3.refs_2_), channel_id=1, source_target_pairs={{0,16},{16,0},{1,17},{17,1},{2,18},{18,2},{3,19},{19,3},{4,20},{20... | collective-permute-start | bytes 393224 | tf_op jit(solution)/shard_map/ppermute | solution.py:157
  49.1 6.2 %collective-permute-start.8 = (bf16[32,2048]{1,0:T(8,128)(2,1)S(1)}, bf16[32,2048]{1,0:T(8,128)(2,1)S(1)}, u32[]{:S(2)}, u32[]{:S(2)}) collective-permute-start(bf16[32,2048]{1,0:T(8,128)(2,1)S(1)} %collective-permute-done.1.refs_4_), channel_id=1, source_target_pairs={{0,16},{16,0},{1,17},{17,1},{2,18},{18,2},{3,19},{19,3},{4,20},{20... | collective-permute-start | bytes 393224 | tf_op jit(solution)/shard_map/ppermute | solution.py:157
  53.2 5.6 %collective-permute-start.4 = (bf16[32,2048]{1,0:T(8,128)(2,1)S(1)}, bf16[32,2048]{1,0:T(8,128)(2,1)S(1)}, u32[]{:S(2)}, u32[]{:S(2)}) collective-permute-start(bf16[32,2048]{1,0:T(8,128)(2,1)S(1)} %collective-permute-done.3.refs_2_), channel_id=1, source_target_pairs={{0,96},{32,0},{64,32},{96,64},{1,97},{33,1},{65,33},{97,65},{2,98}... | collective-permute-start | bytes 393224 | tf_op jit(solution)/shard_map/ppermute | solution.py:161
  53.2 5.7 %collective-permute-start.2 = (bf16[32,2048]{1,0:T(8,128)(2,1)S(1)}, bf16[32,2048]{1,0:T(8,128)(2,1)S(1)}, u32[]{:S(2)}, u32[]{:S(2)}) collective-permute-start(bf16[32,2048]{1,0:T(8,128)(2,1)S(1)} %collective-permute-done.1.refs_4_), channel_id=1, source_target_pairs={{0,128},{128,0},{1,129},{129,1},{2,130},{130,2},{3,131},{131,3},{4... | collective-permute-start | bytes 393224 | tf_op jit(solution)/shard_map/ppermute | solution.py:157
  55.0 6.7 %collective-permute-start.5 = (bf16[32,2048]{1,0:T(8,128)(2,1)S(1)}, bf16[32,2048]{1,0:T(8,128)(2,1)S(1)}, u32[]{:S(2)}, u32[]{:S(2)}) collective-permute-start(bf16[32,2048]{1,0:T(8,128)(2,1)S(1)} %collective-permute-done.refs_0_), channel_id=1, source_target_pairs={{0,128},{128,0},{1,129},{129,1},{2,130},{130,2},{3,131},{131,3},{4... | collective-permute-start | bytes 393224 | tf_op jit(solution)/shard_map/ppermute | solution.py:157
  61.7 1.6 %collective-permute-start.11 = (bf16[32,2048]{1,0:T(8,128)(2,1)S(1)}, bf16[32,2048]{1,0:T(8,128)(2,1)S(1)}, u32[]{:S(2)}, u32[]{:S(2)}) collective-permute-start(bf16[32,2048]{1,0:T(8,128)(2,1)S(1)} %collective-permute-done.refs_0_), channel_id=1, source_target_pairs={{0,16},{16,0},{1,17},{17,1},{2,18},{18,2},{3,19},{19,3},{4,20},{20... | collective-permute-start | bytes 393224 | tf_op jit(solution)/shard_map/ppermute | solution.py:157
  62.3 1.3 %collective-permute-start.12 = (bf16[32,2048]{1,0:T(8,128)(2,1)S(1)}, bf16[32,2048]{1,0:T(8,128)(2,1)S(1)}, u32[]{:S(2)}, u32[]{:S(2)}) collective-permute-start(bf16[32,2048]{1,0:T(8,128)(2,1)S(1)} %collective-permute-done.2.refs_2_), channel_id=1, source_target_pairs={{0,16},{16,0},{1,17},{17,1},{2,18},{18,2},{3,19},{19,3},{4,20},{20... | collective-permute-start | bytes 393224 | tf_op jit(solution)/shard_map/ppermute | solution.py:157
  62.3 1.5 %collective-permute-start.13 = (bf16[32,2048]{1,0:T(8,128)(2,1)S(1)}, bf16[32,2048]{1,0:T(8,128)(2,1)S(1)}, u32[]{:S(2)}, u32[]{:S(2)}) collective-permute-start(bf16[32,2048]{1,0:T(8,128)(2,1)S(1)} %collective-permute-done.4.refs_4_), channel_id=1, source_target_pairs={{0,16},{16,0},{1,17},{17,1},{2,18},{18,2},{3,19},{19,3},{4,20},{20... | collective-permute-start | bytes 393224 | tf_op jit(solution)/shard_map/ppermute | solution.py:157
  62.8 1.3 %collective-permute-start.14 = (bf16[32,2048]{1,0:T(8,128)(2,1)S(1)}, bf16[32,2048]{1,0:T(8,128)(2,1)S(1)}, u32[]{:S(2)}, u32[]{:S(2)}) collective-permute-start(bf16[32,2048]{1,0:T(8,128)(2,1)S(1)} %collective-permute-done.5.refs_6_), channel_id=1, source_target_pairs={{0,16},{16,0},{1,17},{17,1},{2,18},{18,2},{3,19},{19,3},{4,20},{20... | collective-permute-start | bytes 393224 | tf_op jit(solution)/shard_map/ppermute | solution.py:157

commit v3 on v2

--- a/solution.py
+++ b/solution.py
@@ -17,6 +17,7 @@
 TOK = 1024
 LANES = OWN * MOST
 F = G * A
+TILE = 512
 BF = jnp.bfloat16
 F32 = jnp.float32
 NT = (((1,), (1,)), ((), ()))
@@ -60,15 +61,15 @@
     group = slot // 256
     inner = slot % 256
     hot = (iota((256, TOK), 0) == inner).astype(F32).astype(BF)
+    mine = (iota((BLK // 2, TOK), 0) == group).astype(F32).astype(BF)
     copies[2].wait()
     copies[3].wait()
     rows = jnp.concatenate([act_ref[0], grad_ref[0]], axis=0)
-    zero = jnp.zeros_like(rows)
+    parts = jnp.concatenate([rows * mine[o : o + 1] for o in range(BLK // 2)], axis=0)
+    got = lax.dot_general(parts, hot, NT, preferred_element_type=F32).astype(BF)
     for o in range(BLK // 2):
-        part = jnp.where(group == o, rows, zero)
-        got = lax.dot_general(part, hot, NT, preferred_element_type=F32).astype(BF)
-        send_ref[2 * o] = got[:, :LANES]
-        send_ref[2 * o + 1] = got[:, LANES:]
+        send_ref[2 * o] = got[o * W : (o + 1) * W, :LANES]
+        send_ref[2 * o + 1] = got[o * W : (o + 1) * W, LANES:]
     for copy in copies[4:]:
         copy.wait()
 
@@ -83,15 +84,17 @@
 
 
 def cond_kernel(recv_ref, po_ref, pi_ref, cond_ref, square_ref):
-    doc = jnp.zeros((G, OWN * A), F32)
-    mask = (iota((OWN * A, LANES), 0) // A) == (iota((OWN * A, LANES), 1) // MOST)
-    wide = jnp.concatenate([mask, mask], axis=1)
-    for s in range(0, BLK, 2):
-        act = jnp.concatenate([recv_ref[s, :A], recv_ref[s + 1, :A]], axis=1)
-        grad = jnp.concatenate([recv_ref[s, A:], recv_ref[s + 1, A:]], axis=1)
-        spread = jnp.concatenate([act] * OWN, axis=0)
-        spread = jnp.where(wide, spread, jnp.zeros_like(spread))
-        doc += lax.dot_general(grad, spread, NT, preferred_element_type=F32)
+    span = OWN // 4
+    wide = BLK * span * MOST
+    mask = (iota((span * A, wide), 0) // A) == (iota((span * A, wide), 1) // MOST % span)
+    docs = []
+    for q in range(4):
+        cols = slice(q * span * MOST, (q + 1) * span * MOST)
+        both = jnp.concatenate([recv_ref[s][:, cols] for s in range(BLK)], axis=1)
+        spread = jnp.concatenate([both[:A]] * span, axis=0)
+        spread = jnp.where(mask, spread, jnp.zeros_like(spread))
+        docs.append(lax.dot_general(both[A:], spread, NT, preferred_element_type=F32))
+    doc = jnp.concatenate(docs, axis=1)
     po_hi, po_lo = split(po_ref[0])
     d_hi, d_lo = split(doc)
     left = dot(
@@ -109,11 +112,13 @@
     pi_hi, pi_lo = split(pi_ref[0])
     pi_hi, pi_lo = block_diagonal(pi_hi), block_diagonal(pi_lo)
     l_hi, l_lo = split(left)
-    outs = []
-    for q in range(OWN * A // 256):
-        cols = slice(q * 256, (q + 1) * 256)
-        outs.append(dot(l_hi[:, cols], pi_hi) + dot(l_lo[:, cols], pi_hi) + dot(l_hi[:, cols], pi_lo))
-    cond = jnp.concatenate(outs, axis=1)
+    def stack(part):
+        return jnp.concatenate([part[:, q * 256 : (q + 1) * 256] for q in range(OWN * A // 256)], axis=0)
+
+    l_hi, l_lo = stack(l_hi), stack(l_lo)
+    both = dot(jnp.concatenate([l_hi, l_lo], axis=0), pi_hi)
+    cond = both[:256] + both[256:] + dot(l_hi, pi_lo)
+    cond = jnp.concatenate([cond[q * G : (q + 1) * G] for q in range(OWN * A // 256)], axis=1)
     cond = jnp.transpose(cond.reshape(G, OWN, A), (1, 0, 2)).reshape(OWN, F)
     cond_ref[...] = cond
     square = jnp.sum(cond * cond, axis=1, keepdims=True)
@@ -130,16 +135,13 @@
     doc_ref[...] = (cond_ref[...] * inverse).astype(BF)
 
 
-def score_kernel(places, *refs):
-    count = len(places)
-    blocks, train_ref, out_hbm, buffer, sem = refs[:count], refs[count], *refs[-3:]
+def score_tiles(places, blocks, tiles, out_hbm, buffer, sem):
     x, y, c = (lax.axis_index(a) for a in BLK_AXES)
     docs = jnp.concatenate([b[...] for b in blocks], axis=0)
-    tile = 512
     copies = []
-    for i in range(buffer.shape[1] // tile):
-        cols = pl.ds(i * tile, tile)
-        buffer[:, cols] = lax.dot_general(docs, train_ref[0, cols, :], NT, preferred_element_type=F32)
+    for i, tile in enumerate(tiles):
+        cols = pl.ds(i * TILE, TILE)
+        buffer[:, cols] = lax.dot_general(docs, tile(), NT, preferred_element_type=F32)
         for j, (dx, dy, dc) in enumerate(places):
             at = (((x ^ dx) * 4 + (y + dy) % 4) * 2 + (c ^ dc)) * OWN
             copy = pltpu.make_async_copy(
@@ -153,6 +155,15 @@
         copy.wait()
 
 
+def tiles_of(train_ref):
+    return [lambda i=i: train_ref[0, i * TILE : (i + 1) * TILE] for i in range(train_ref.shape[1] // TILE)]
+
+
+def score_kernel(places, count, *refs):
+    blocks, train_ref, (out_hbm, buffer, sem) = refs[:count], refs[count], refs[-3:]
+    score_tiles(places, blocks, tiles_of(train_ref), out_hbm, buffer, sem)
+
+
 def swap(x, axis):
     return lax.ppermute(x, axis, [(0, 1), (1, 0)])
 
@@ -161,23 +172,22 @@
     return lax.ppermute(x, "y", [(i, (i + by) % 4) for i in range(4)])
 
 
-def score(name, places, blocks, train, out=None):
+def score(places, blocks, train, *out):
+    hbm = pl.BlockSpec(memory_space=pltpu.HBM)
     rows = train.shape[1]
-    hbm = pl.BlockSpec(memory_space=pltpu.HBM)
-    more = () if out is None else (out,)
     return pl.pallas_call(
-        functools.partial(score_kernel, places),
+        functools.partial(score_kernel, places, len(blocks)),
         out_shape=pltpu.HBM((1, DOCS, rows), F32),
-        in_specs=[VM] * (len(blocks) + 1) + [hbm] * len(more),
+        in_specs=[VM] * (len(blocks) + 1) + [hbm] * len(out),
         out_specs=hbm,
         scratch_shapes=[
-            pltpu.VMEM((len(blocks) * OWN, rows), F32),
-            pltpu.SemaphoreType.DMA((rows // 512, len(blocks))),
+            pltpu.VMEM((len(places) * OWN, rows), F32),
+            pltpu.SemaphoreType.DMA((rows // TILE, len(places))),
         ],
-        input_output_aliases={len(blocks) + 1: 0} if more else {},
-        name=name,
+        input_output_aliases={len(blocks) + 1: 0} if out else {},
+        name="far" if out else "near",
         compiler_params=room(8),
-    )(*blocks, train, *more)
+    )(*blocks, train, *out)
 
 
 def pair(block):
@@ -216,7 +226,7 @@
             jax.ShapeDtypeStruct((BLK, 8, 128), F32),
         ),
         in_specs=[VM] * 3,
-        out_specs=(VM, VM),
+        out_specs=[VM] * 2,
         name="condition",
         compiler_params=room(16),
     )(received, pre_out, pre_in)
@@ -230,13 +240,14 @@
         compiler_params=room(2),
     )(cond, squares)
     side, above, below, over = swap(doc, "xl"), turn(doc, 1), turn(doc, -1), turn(doc, 2)
+    side_above, side_below, side_over = swap(above, "xl"), turn(side, -1), swap(over, "xl")
+    doc, side, above, below, over = lax.optimization_barrier((doc, side, above, below, over))
     near = pair(doc) + pair(side) + pair(above) + pair(below)
-    side_above, side_below, side_over = swap(above, "xl"), turn(side, -1), swap(over, "xl")
-    out = score("near", label((0, 0), (1, 0), (0, 3), (0, 1)), near, train)
-    far = lax.optimization_barrier((over, side_above, side_below, side_over, out))
-    over, side_above, side_below, side_over, out = far
-    far = pair(over) + pair(side_above) + pair(side_below) + pair(side_over)
-    return score("far", label((0, 2), (1, 3), (1, 1), (1, 2)), far, train, out)
+    out = score(label((0, 0), (1, 0), (0, 3), (0, 1)), near, train)
+    far = pair(over)
+    side_above, side_below, side_over, out = lax.optimization_barrier((side_above, side_below, side_over, out))
+    far += pair(side_above) + pair(side_below) + pair(side_over)
+    return score(label((0, 2), (1, 3), (1, 1), (1, 2)), far, train, out)
 
 
 def solution(mesh):

time: 67.9 us -> 65 us (0.957)
  starting transfers between devices: 15.8 us -> 11 us
  waiting for transfers between devices: 4.29 us -> 7.29 us
  Pallas kernels: 13.1 us -> 12.1 us
    ppermute x4, waiting for transfers between devices: 0.01 us -> 6.25 us  [turn(): return lax.ppermute(x, 'y', [(i, (i + by) % 4) for i in range(4)])]
    ppermute x11, starting transfers between devices: 13 us -> 7 us  [swap(): return lax.ppermute(x, axis, [(0, 1), (1, 0)])]
    ppermute x11, waiting for transfers between devices: 4.28 us -> 1.04 us  [swap(): return lax.ppermute(x, axis, [(0, 1), (1, 0)])]
    ppermute x4, starting transfers between devices: 2.85 us -> 3.96 us  [turn(): return lax.ppermute(x, 'y', [(i, (i + by) % 4) for i in range(4)])]
    pallas_call x1, Pallas kernels: 2.46 us -> 1.47 us  [body(): pl.pallas_call(cond_kernel, out_shape=(jax.ShapeDtypeStruct((OWN, F), F32...]
where the time goes in v3:
time: 65 us; the launch traced here: 64.8 us
  blocking collectives  34.2 us (53%)
  Pallas kernels  12.1 us (19%)
  starting transfers between devices  11 us (17%)
  waiting for transfers between devices  7.29 us (11%)
    all_to_all x1, blocking collectives, body(): lax.all_to_all(squares, MOD_AXES, split_axis=0, concat_axis=0, tiled=True)  19.1 us
    all_to_all x1, blocking collectives, body(): lax.all_to_all(send, BLK_AXES, split_axis=0, concat_axis=0, tiled=True)  15.1 us
    ppermute x11, starting transfers between devices, swap(): return lax.ppermute(x, axis, [(0, 1), (1, 0)])  7 us
    pallas_call x2, Pallas kernels, score(): pl.pallas_call(functools.partial(score_kernel, places, len(blocks)), out_...  6.85 us
    ppermute x4, waiting for transfers between devices, turn(): return lax.ppermute(x, 'y', [(i, (i + by) % 4) for i in range(4)])  6.25 us
    ppermute x4, starting transfers between devices, turn(): return lax.ppermute(x, 'y', [(i, (i + by) % 4) for i in range(4)])  3.96 us
    pallas_call x1, Pallas kernels, body(): pl.pallas_call(slot_kernel, out_shape=(jax.ShapeDtypeStruct((BLK, W, LANE...  3.63 us
    pallas_call x1, Pallas kernels, body(): pl.pallas_call(cond_kernel, out_shape=(jax.ShapeDtypeStruct((OWN, F), F32...  1.47 us
  transfers between devices with their start and end apart: 15, of which 6 were waited for; matrix products, arithmetic and copies ran while one was open for 0% of the time, Pallas kernels for 5%

profile of v3, /device:TPU:1, one launch (start us, length us, event | category | flops | bytes accessed | tf_op | source)
XLA Modules:
  0.0 64.8 jit_solution(17377523530894846802)
XLA Ops:
  0.0 3.6 %slots.1 = (bf16[16,96,128]{2,1,0:T(8,128)(2,1)S(1)}, f32[1,64,64]{2,1,0:T(8,128)S(1)}, f32[1,32,32]{2,1,0:T(8,128)S(1)}, bf16[1,2048,2048]{2,1,0:T(8,128)(2,1)S(1)}) custom-call(bf16[1,32,1024]{2,1,0:T(8,128)(2,1)} %act_hbm.1, bf16[1,64,1024]{2,1,0:T(8,128)(2,1)} %grad_hbm.1, s32[1,1024]{1,0:T(1,128)} %bitcast.2, s32[1,512]{1,0:T(1,128)} %bitcast.3, ...), custom_call_target="tpu_custom_call" | custom-call | tf_op jit(solution)/shard_map/slots/pallas_call | solution.py:206
  3.6 15.1 %all_to_all.10.recv_ref = bf16[16,96,128]{2,1,0:T(8,128)(2,1)S(1)} all-to-all(bf16[16,96,128]{2,1,0:T(8,128)(2,1)S(1)} %get-tuple-element.20), channel_id=1, replica_groups=mesh['xl'=2,'y'=4,'core'=2,'xh'=2,'z'=8] {'xl','y','core'}, dimensions={0} | all-to-all | bytes 786432 | tf_op jit(solution)/shard_map/all_to_all | solution.py:221
  18.7 1.5 %condition.1 = (f32[32,2048]{1,0:T(8,128)S(1)}, f32[16,8,128]{2,1,0:T(8,128)S(1)}) custom-call(bf16[16,96,128]{2,1,0:T(8,128)(2,1)S(1)} %all_to_all.10.recv_ref, f32[1,64,64]{2,1,0:T(8,128)S(1)} %get-tuple-element.21.po_ref, f32[1,32,32]{2,1,0:T(8,128)S(1)} %get-tuple-element.22.pi_ref), custom_call_target="tpu_custom_call" | custom-call | tf_op jit(solution)/shard_map/condition/pallas_call | solution.py:222
  20.2 19.1 %all_to_all.11.squares_ref = f32[16,8,128]{2,1,0:T(8,128)S(1)} all-to-all(f32[16,8,128]{2,1,0:T(8,128)S(1)} %get-tuple-element.24), channel_id=1, replica_groups=mesh['xl'=2,'y'=4,'core'=2,'xh'=2,'z'=8] {'xh','z'}, dimensions={0} | all-to-all | bytes 131072 | tf_op jit(solution)/shard_map/all_to_all | solution.py:233
  39.4 0.2 scale.1.refs_0_
  39.5 1.1 %collective-permute-start.3 = (bf16[32,2048]{1,0:T(8,128)(2,1)S(1)}, bf16[32,2048]{1,0:T(8,128)(2,1)S(1)}, u32[]{:S(2)}, u32[]{:S(2)}) collective-permute-start(bf16[32,2048]{1,0:T(8,128)(2,1)S(1)} %scale.1.refs_0_), channel_id=1, source_target_pairs={{0,64},{32,96},{64,0},{96,32},{1,65},{33,97},{65,1},{97,33},{2,66}... | collective-permute-start | bytes 393224 | tf_op jit(solution)/shard_map/ppermute | solution.py:172
  40.7 1.3 %collective-permute-start.2 = (bf16[32,2048]{1,0:T(8,128)(2,1)S(1)}, bf16[32,2048]{1,0:T(8,128)(2,1)S(1)}, u32[]{:S(2)}, u32[]{:S(2)}) collective-permute-start(bf16[32,2048]{1,0:T(8,128)(2,1)S(1)} %scale.1.refs_0_), channel_id=1, source_target_pairs={{0,96},{32,0},{64,32},{96,64},{1,97},{33,1},{65,33},{97,65},{2,98}... | collective-permute-start | bytes 393224 | tf_op jit(solution)/shard_map/ppermute | solution.py:172
  41.9 0.2 collective-permute-start.1
  42.2 0.5 collective-permute-start
  42.7 2.3 %collective-permute-done.3.refs_0_ = bf16[32,2048]{1,0:T(8,128)(2,1)S(1)} collective-permute-done((bf16[32,2048]{1,0:T(8,128)(2,1)S(1)}, bf16[32,2048]{1,0:T(8,128)(2,1)S(1)}, u32[]{:S(2)}, u32[]{:S(2)}) %collective-permute-start.3) | collective-permute-done | bytes 131104 | tf_op jit(solution)/shard_map/ppermute | solution.py:172
  44.9 1.3 %collective-permute-done.2.refs_6_ = bf16[32,2048]{1,0:T(8,128)(2,1)S(1)} collective-permute-done((bf16[32,2048]{1,0:T(8,128)(2,1)S(1)}, bf16[32,2048]{1,0:T(8,128)(2,1)S(1)}, u32[]{:S(2)}, u32[]{:S(2)}) %collective-permute-start.2) | collective-permute-done | bytes 131104 | tf_op jit(solution)/shard_map/ppermute | solution.py:172
  46.2 2.7 %collective-permute-done.1.refs_4_ = bf16[32,2048]{1,0:T(8,128)(2,1)S(1)} collective-permute-done((bf16[32,2048]{1,0:T(8,128)(2,1)S(1)}, bf16[32,2048]{1,0:T(8,128)(2,1)S(1)}, u32[]{:S(2)}, u32[]{:S(2)}) %collective-permute-start.1) | collective-permute-done | bytes 131104 | tf_op jit(solution)/shard_map/ppermute | solution.py:172
  48.9 0.0 collective-permute-done.refs_2_
  48.9 1.6 %collective-permute-start.8 = (bf16[32,2048]{1,0:T(8,128)(2,1)S(1)}, bf16[32,2048]{1,0:T(8,128)(2,1)S(1)}, u32[]{:S(2)}, u32[]{:S(2)}) collective-permute-start(bf16[32,2048]{1,0:T(8,128)(2,1)S(1)} %scale.1.refs_0_), channel_id=1, source_target_pairs={{0,16},{16,0},{1,17},{17,1},{2,18},{18,2},{3,19},{19,3},{4,20},{20... | collective-permute-start | bytes 393224 | tf_op jit(solution)/shard_map/ppermute | solution.py:168
  50.5 0.0 collective-permute-start.9
  50.5 0.5 collective-permute-start.10
  51.0 0.0 collective-permute-start.11
  51.0 0.5 collective-permute-start.7
  51.5 0.0 collective-permute-done.8.refs_1_
  51.5 0.9 %collective-permute-start.5 = (bf16[32,2048]{1,0:T(8,128)(2,1)S(1)}, bf16[32,2048]{1,0:T(8,128)(2,1)S(1)}, u32[]{:S(2)}, u32[]{:S(2)}) collective-permute-start(bf16[32,2048]{1,0:T(8,128)(2,1)S(1)} %collective-permute-done.1.refs_4_), channel_id=1, source_target_pairs={{0,128},{128,0},{1,129},{129,1},{2,130},{130,2},{3,131},{131,3},{4... | collective-permute-start | bytes 393224 | tf_op jit(solution)/shard_map/ppermute | solution.py:168
  52.5 0.0 collective-permute-done.9.refs_3_
  52.5 1.4 %collective-permute-start.6 = (bf16[32,2048]{1,0:T(8,128)(2,1)S(1)}, bf16[32,2048]{1,0:T(8,128)(2,1)S(1)}, u32[]{:S(2)}, u32[]{:S(2)}) collective-permute-start(bf16[32,2048]{1,0:T(8,128)(2,1)S(1)} %collective-permute-done.refs_2_), channel_id=1, source_target_pairs={{0,96},{32,0},{64,32},{96,64},{1,97},{33,1},{65,33},{97,65},{2,98}... | collective-permute-start | bytes 393224 | tf_op jit(solution)/shard_map/ppermute | solution.py:172
  53.8 0.0 collective-permute-done.10.refs_5_
  53.8 1.3 %collective-permute-start.4 = (bf16[32,2048]{1,0:T(8,128)(2,1)S(1)}, bf16[32,2048]{1,0:T(8,128)(2,1)S(1)}, u32[]{:S(2)}, u32[]{:S(2)}) collective-permute-start(bf16[32,2048]{1,0:T(8,128)(2,1)S(1)} %collective-permute-done.3.refs_0_), channel_id=1, source_target_pairs={{0,16},{16,0},{1,17},{17,1},{2,18},{18,2},{3,19},{19,3},{4,20},{20... | collective-permute-start | bytes 393224 | tf_op jit(solution)/shard_map/ppermute | solution.py:168
  55.2 0.0 collective-permute-done.11.refs_7_
  55.2 3.4 %near.1.refs_9_ = f32[1,512,2048]{2,1,0:T(8,128)} custom-call(bf16[32,2048]{1,0:T(8,128)(2,1)S(1)} %scale.1.refs_0_, bf16[32,2048]{1,0:T(8,128)(2,1)S(1)} %collective-permute-done.8.refs_1_, bf16[32,2048]{1,0:T(8,128)(2,1)S(1)} %collective-permute-done.refs_2_, bf16[32,2048]{1,0:T(8,128)(2,1)S(1)} %collective-permute-done.9.refs_3_, ...), custom_call_target="tpu_custom_call" | custom-call | tf_op jit(solution)/shard_map/near/pallas_call | solution.py:178
  58.6 0.0 collective-permute-done.7.refs_6_
  58.6 0.0 collective-permute-done.5.refs_2_
  58.6 0.0 collective-permute-done.6.refs_4_
  58.6 1.1 %collective-permute-start.12 = (bf16[32,2048]{1,0:T(8,128)(2,1)S(1)}, bf16[32,2048]{1,0:T(8,128)(2,1)S(1)}, u32[]{:S(2)}, u32[]{:S(2)}) collective-permute-start(bf16[32,2048]{1,0:T(8,128)(2,1)S(1)} %collective-permute-done.5.refs_2_), channel_id=1, source_target_pairs={{0,16},{16,0},{1,17},{17,1},{2,18},{18,2},{3,19},{19,3},{4,20},{20... | collective-permute-start | bytes 393224 | tf_op jit(solution)/shard_map/ppermute | solution.py:168
  59.7 0.0 collective-permute-start.13
  59.7 0.5 collective-permute-start.14
  60.2 0.0 collective-permute-done.4.refs_1_
  60.2 0.5 collective-permute-done.12.refs_3_
  60.7 0.4 collective-permute-done.13.refs_5_
  61.1 0.2 collective-permute-done.14.refs_7_
  61.3 3.4 %far.1 = f32[1,512,2048]{2,1,0:T(8,128)} custom-call(bf16[32,2048]{1,0:T(8,128)(2,1)S(1)} %collective-permute-done.3.refs_0_, bf16[32,2048]{1,0:T(8,128)(2,1)S(1)} %collective-permute-done.4.refs_1_, bf16[32,2048]{1,0:T(8,128)(2,1)S(1)} %collective-permute-done.5.refs_2_, ...), custom_call_target="tpu_custom_call", output_to_operand_aliasing={{}: (9, {})} | custom-call | tf_op jit(solution)/shard_map/far/pallas_call | solution.py:178
Async XLA Ops:
  39.5 5.4 %collective-permute-start.3 = (bf16[32,2048]{1,0:T(8,128)(2,1)S(1)}, bf16[32,2048]{1,0:T(8,128)(2,1)S(1)}, u32[]{:S(2)}, u32[]{:S(2)}) collective-permute-start(bf16[32,2048]{1,0:T(8,128)(2,1)S(1)} %scale.1.refs_0_), channel_id=1, source_target_pairs={{0,64},{32,96},{64,0},{96,32},{1,65},{33,97},{65,1},{97,33},{2,66}... | collective-permute-start | bytes 393224 | tf_op jit(solution)/shard_map/ppermute | solution.py:172
  40.7 5.6 %collective-permute-start.2 = (bf16[32,2048]{1,0:T(8,128)(2,1)S(1)}, bf16[32,2048]{1,0:T(8,128)(2,1)S(1)}, u32[]{:S(2)}, u32[]{:S(2)}) collective-permute-start(bf16[32,2048]{1,0:T(8,128)(2,1)S(1)} %scale.1.refs_0_), channel_id=1, source_target_pairs={{0,96},{32,0},{64,32},{96,64},{1,97},{33,1},{65,33},{97,65},{2,98}... | collective-permute-start | bytes 393224 | tf_op jit(solution)/shard_map/ppermute | solution.py:172
  41.9 7.0 %collective-permute-start.1 = (bf16[32,2048]{1,0:T(8,128)(2,1)S(1)}, bf16[32,2048]{1,0:T(8,128)(2,1)S(1)}, u32[]{:S(2)}, u32[]{:S(2)}) collective-permute-start(bf16[32,2048]{1,0:T(8,128)(2,1)S(1)} %scale.1.refs_0_), channel_id=1, source_target_pairs={{0,32},{32,64},{64,96},{96,0},{1,33},{33,65},{65,97},{97,1},{2,34}... | collective-permute-start | bytes 393224 | tf_op jit(solution)/shard_map/ppermute | solution.py:172
  42.2 6.8 %collective-permute-start = (bf16[32,2048]{1,0:T(8,128)(2,1)S(1)}, bf16[32,2048]{1,0:T(8,128)(2,1)S(1)}, u32[]{:S(2)}, u32[]{:S(2)}) collective-permute-start(bf16[32,2048]{1,0:T(8,128)(2,1)S(1)} %scale.1.refs_0_), channel_id=1, source_target_pairs={{0,128},{128,0},{1,129},{129,1},{2,130},{130,2},{3,131},{131,3},{4... | collective-permute-start | bytes 393224 | tf_op jit(solution)/shard_map/ppermute | solution.py:168
  48.9 2.6 %collective-permute-start.8 = (bf16[32,2048]{1,0:T(8,128)(2,1)S(1)}, bf16[32,2048]{1,0:T(8,128)(2,1)S(1)}, u32[]{:S(2)}, u32[]{:S(2)}) collective-permute-start(bf16[32,2048]{1,0:T(8,128)(2,1)S(1)} %scale.1.refs_0_), channel_id=1, source_target_pairs={{0,16},{16,0},{1,17},{17,1},{2,18},{18,2},{3,19},{19,3},{4,20},{20... | collective-permute-start | bytes 393224 | tf_op jit(solution)/shard_map/ppermute | solution.py:168
  50.5 2.0 %collective-permute-start.9 = (bf16[32,2048]{1,0:T(8,128)(2,1)S(1)}, bf16[32,2048]{1,0:T(8,128)(2,1)S(1)}, u32[]{:S(2)}, u32[]{:S(2)}) collective-permute-start(bf16[32,2048]{1,0:T(8,128)(2,1)S(1)} %collective-permute-done.refs_2_), channel_id=1, source_target_pairs={{0,16},{16,0},{1,17},{17,1},{2,18},{18,2},{3,19},{19,3},{4,20},{20... | collective-permute-start | bytes 393224 | tf_op jit(solution)/shard_map/ppermute | solution.py:168
  50.5 3.3 %collective-permute-start.10 = (bf16[32,2048]{1,0:T(8,128)(2,1)S(1)}, bf16[32,2048]{1,0:T(8,128)(2,1)S(1)}, u32[]{:S(2)}, u32[]{:S(2)}) collective-permute-start(bf16[32,2048]{1,0:T(8,128)(2,1)S(1)} %collective-permute-done.1.refs_4_), channel_id=1, source_target_pairs={{0,16},{16,0},{1,17},{17,1},{2,18},{18,2},{3,19},{19,3},{4,20},{20... | collective-permute-start | bytes 393224 | tf_op jit(solution)/shard_map/ppermute | solution.py:168
  51.0 4.2 %collective-permute-start.11 = (bf16[32,2048]{1,0:T(8,128)(2,1)S(1)}, bf16[32,2048]{1,0:T(8,128)(2,1)S(1)}, u32[]{:S(2)}, u32[]{:S(2)}) collective-permute-start(bf16[32,2048]{1,0:T(8,128)(2,1)S(1)} %collective-permute-done.2.refs_6_), channel_id=1, source_target_pairs={{0,16},{16,0},{1,17},{17,1},{2,18},{18,2},{3,19},{19,3},{4,20},{20... | collective-permute-start | bytes 393224 | tf_op jit(solution)/shard_map/ppermute | solution.py:168
  51.0 7.6 %collective-permute-start.7 = (bf16[32,2048]{1,0:T(8,128)(2,1)S(1)}, bf16[32,2048]{1,0:T(8,128)(2,1)S(1)}, u32[]{:S(2)}, u32[]{:S(2)}) collective-permute-start(bf16[32,2048]{1,0:T(8,128)(2,1)S(1)} %collective-permute-done.3.refs_0_), channel_id=1, source_target_pairs={{0,128},{128,0},{1,129},{129,1},{2,130},{130,2},{3,131},{131,3},{4... | collective-permute-start | bytes 393224 | tf_op jit(solution)/shard_map/ppermute | solution.py:168
  51.5 7.1 %collective-permute-start.5 = (bf16[32,2048]{1,0:T(8,128)(2,1)S(1)}, bf16[32,2048]{1,0:T(8,128)(2,1)S(1)}, u32[]{:S(2)}, u32[]{:S(2)}) collective-permute-start(bf16[32,2048]{1,0:T(8,128)(2,1)S(1)} %collective-permute-done.1.refs_4_), channel_id=1, source_target_pairs={{0,128},{128,0},{1,129},{129,1},{2,130},{130,2},{3,131},{131,3},{4... | collective-permute-start | bytes 393224 | tf_op jit(solution)/shard_map/ppermute | solution.py:168
  52.5 6.2 %collective-permute-start.6 = (bf16[32,2048]{1,0:T(8,128)(2,1)S(1)}, bf16[32,2048]{1,0:T(8,128)(2,1)S(1)}, u32[]{:S(2)}, u32[]{:S(2)}) collective-permute-start(bf16[32,2048]{1,0:T(8,128)(2,1)S(1)} %collective-permute-done.refs_2_), channel_id=1, source_target_pairs={{0,96},{32,0},{64,32},{96,64},{1,97},{33,1},{65,33},{97,65},{2,98}... | collective-permute-start | bytes 393224 | tf_op jit(solution)/shard_map/ppermute | solution.py:172
  53.8 6.4 %collective-permute-start.4 = (bf16[32,2048]{1,0:T(8,128)(2,1)S(1)}, bf16[32,2048]{1,0:T(8,128)(2,1)S(1)}, u32[]{:S(2)}, u32[]{:S(2)}) collective-permute-start(bf16[32,2048]{1,0:T(8,128)(2,1)S(1)} %collective-permute-done.3.refs_0_), channel_id=1, source_target_pairs={{0,16},{16,0},{1,17},{17,1},{2,18},{18,2},{3,19},{19,3},{4,20},{20... | collective-permute-start | bytes 393224 | tf_op jit(solution)/shard_map/ppermute | solution.py:168
  58.6 2.1 %collective-permute-start.12 = (bf16[32,2048]{1,0:T(8,128)(2,1)S(1)}, bf16[32,2048]{1,0:T(8,128)(2,1)S(1)}, u32[]{:S(2)}, u32[]{:S(2)}) collective-permute-start(bf16[32,2048]{1,0:T(8,128)(2,1)S(1)} %collective-permute-done.5.refs_2_), channel_id=1, source_target_pairs={{0,16},{16,0},{1,17},{17,1},{2,18},{18,2},{3,19},{19,3},{4,20},{20... | collective-permute-start | bytes 393224 | tf_op jit(solution)/shard_map/ppermute | solution.py:168
  59.7 1.3 %collective-permute-start.13 = (bf16[32,2048]{1,0:T(8,128)(2,1)S(1)}, bf16[32,2048]{1,0:T(8,128)(2,1)S(1)}, u32[]{:S(2)}, u32[]{:S(2)}) collective-permute-start(bf16[32,2048]{1,0:T(8,128)(2,1)S(1)} %collective-permute-done.6.refs_4_), channel_id=1, source_target_pairs={{0,16},{16,0},{1,17},{17,1},{2,18},{18,2},{3,19},{19,3},{4,20},{20... | collective-permute-start | bytes 393224 | tf_op jit(solution)/shard_map/ppermute | solution.py:168
  59.7 1.5 %collective-permute-start.14 = (bf16[32,2048]{1,0:T(8,128)(2,1)S(1)}, bf16[32,2048]{1,0:T(8,128)(2,1)S(1)}, u32[]{:S(2)}, u32[]{:S(2)}) collective-permute-start(bf16[32,2048]{1,0:T(8,128)(2,1)S(1)} %collective-permute-done.7.refs_6_), channel_id=1, source_target_pairs={{0,16},{16,0},{1,17},{17,1},{2,18},{18,2},{3,19},{19,3},{4,20},{20... | collective-permute-start | bytes 393224 | tf_op jit(solution)/shard_map/ppermute | solution.py:168

commit v4 on v3

--- a/solution.py
+++ b/solution.py
@@ -124,14 +124,13 @@
     square = jnp.sum(cond * cond, axis=1, keepdims=True)
     row = jnp.transpose(jnp.broadcast_to(square, (OWN, 128)))[:8]
     row = jnp.concatenate([row, jnp.zeros((8, 128 - OWN), F32)], axis=1)
-    for m in range(BLK):
-        square_ref[m] = row
+    square_ref[...] = jnp.concatenate([row] * (BLK // 8), axis=0)
 
 
 def scale_kernel(cond_ref, squares_ref, doc_ref):
-    total = jnp.sum(squares_ref[...], axis=0)
+    total = jnp.sum(squares_ref[...], axis=0, keepdims=True)
     inverse = 1.0 / jnp.sqrt(total + 1e-6)
-    inverse = jnp.transpose(jnp.broadcast_to(inverse[:1], (8, 128)))[:OWN, :1]
+    inverse = jnp.transpose(jnp.broadcast_to(inverse, (8, 128)))[:OWN, :1]
     doc_ref[...] = (cond_ref[...] * inverse).astype(BF)
 
 
@@ -223,7 +222,7 @@
         cond_kernel,
         out_shape=(
             jax.ShapeDtypeStruct((OWN, F), F32),
-            jax.ShapeDtypeStruct((BLK, 8, 128), F32),
+            jax.ShapeDtypeStruct((BLK, 128), F32),
         ),
         in_specs=[VM] * 3,
         out_specs=[VM] * 2,
@@ -241,7 +240,7 @@
     )(cond, squares)
     side, above, below, over = swap(doc, "xl"), turn(doc, 1), turn(doc, -1), turn(doc, 2)
     side_above, side_below, side_over = swap(above, "xl"), turn(side, -1), swap(over, "xl")
-    doc, side, above, below, over = lax.optimization_barrier((doc, side, above, below, over))
+    side, above, below, over = lax.optimization_barrier((side, above, below, over))
     near = pair(doc) + pair(side) + pair(above) + pair(below)
     out = score(label((0, 0), (1, 0), (0, 3), (0, 1)), near, train)
     far = pair(over)

time: 65 us -> 65 us (level)
  waiting for transfers between devices: 7.29 us -> 5.25 us
  starting transfers between devices: 11 us -> 13 us
    ppermute x4, waiting for transfers between devices: 6.25 us -> 3.3 us  [turn(): return lax.ppermute(x, 'y', [(i, (i + by) % 4) for i in range(4)])]
    ppermute x11, starting transfers between devices: 7 us -> 9.14 us  [swap(): return lax.ppermute(x, axis, [(0, 1), (1, 0)])]
    ppermute x11, waiting for transfers between devices: 1.04 us -> 1.94 us  [swap(): return lax.ppermute(x, axis, [(0, 1), (1, 0)])]
where the time goes in v4:
time: 65 us; the launch traced here: 64.8 us
  blocking collectives  34.2 us (53%)
  starting transfers between devices  13 us (20%)
  Pallas kernels  12.1 us (19%)
  waiting for transfers between devices  5.25 us (8%)
    all_to_all x1, blocking collectives, body(): lax.all_to_all(squares, MOD_AXES, split_axis=0, concat_axis=0, tiled=True)  19.1 us
    all_to_all x1, blocking collectives, body(): lax.all_to_all(send, BLK_AXES, split_axis=0, concat_axis=0, tiled=True)  15.1 us
    ppermute x11, starting transfers between devices, swap(): return lax.ppermute(x, axis, [(0, 1), (1, 0)])  9.14 us
    pallas_call x2, Pallas kernels, score(): pl.pallas_call(functools.partial(score_kernel, places, len(blocks)), out_...  6.84 us
    ppermute x4, starting transfers between devices, turn(): return lax.ppermute(x, 'y', [(i, (i + by) % 4) for i in range(4)])  3.9 us
    pallas_call x1, Pallas kernels, body(): pl.pallas_call(slot_kernel, out_shape=(jax.ShapeDtypeStruct((BLK, W, LANE...  3.63 us
    ppermute x4, waiting for transfers between devices, turn(): return lax.ppermute(x, 'y', [(i, (i + by) % 4) for i in range(4)])  3.3 us
    ppermute x11, waiting for transfers between devices, swap(): return lax.ppermute(x, axis, [(0, 1), (1, 0)])  1.94 us
  transfers between devices with their start and end apart: 15, of which 6 were waited for; matrix products, arithmetic and copies ran while one was open for 0% of the time, Pallas kernels for 5%

profile of v4, /device:TPU:1, one launch (start us, length us, event | category | flops | bytes accessed | tf_op | source)
XLA Modules:
  0.0 64.8 jit_solution(11968614969381381246)
XLA Ops:
  0.0 3.6 %slots.1 = (bf16[16,96,128]{2,1,0:T(8,128)(2,1)S(1)}, f32[1,64,64]{2,1,0:T(8,128)S(1)}, f32[1,32,32]{2,1,0:T(8,128)S(1)}, bf16[1,2048,2048]{2,1,0:T(8,128)(2,1)S(1)}) custom-call(bf16[1,32,1024]{2,1,0:T(8,128)(2,1)} %act_hbm.1, bf16[1,64,1024]{2,1,0:T(8,128)(2,1)} %grad_hbm.1, s32[1,1024]{1,0:T(1,128)} %bitcast.8, s32[1,512]{1,0:T(1,128)} %bitcast.9, ...), custom_call_target="tpu_custom_call" | custom-call | tf_op jit(solution)/shard_map/slots/pallas_call | solution.py:205
  3.6 15.1 %all_to_all.16.recv_ref = bf16[16,96,128]{2,1,0:T(8,128)(2,1)S(1)} all-to-all(bf16[16,96,128]{2,1,0:T(8,128)(2,1)S(1)} %get-tuple-element.19), channel_id=1, replica_groups=mesh['xl'=2,'y'=4,'core'=2,'xh'=2,'z'=8] {'xl','y','core'}, dimensions={0} | all-to-all | bytes 786432 | tf_op jit(solution)/shard_map/all_to_all | solution.py:220
  18.7 1.5 %condition.1 = (f32[32,2048]{1,0:T(8,128)S(1)}, f32[16,128]{1,0:T(8,128)S(1)}) custom-call(bf16[16,96,128]{2,1,0:T(8,128)(2,1)S(1)} %all_to_all.16.recv_ref, f32[1,64,64]{2,1,0:T(8,128)S(1)} %get-tuple-element.20.po_ref, f32[1,32,32]{2,1,0:T(8,128)S(1)} %get-tuple-element.21.pi_ref), custom_call_target="tpu_custom_call" | custom-call | tf_op jit(solution)/shard_map/condition/pallas_call | solution.py:221
  20.2 19.1 %all_to_all.17 = f32[16,1,128]{2,1,0:T(1,128)S(1)} all-to-all(f32[16,1,128]{2,1,0:T(1,128)S(1)} %bitcast.7), channel_id=1, replica_groups=mesh['xl'=2,'y'=4,'core'=2,'xh'=2,'z'=8] {'xh','z'}, dimensions={0} | all-to-all | bytes 16384 | tf_op jit(solution)/shard_map/all_to_all | solution.py:232
  39.3 0.2 scale.1.refs_0_
  39.4 1.2 %collective-permute-start.3 = (bf16[32,2048]{1,0:T(8,128)(2,1)S(1)}, bf16[32,2048]{1,0:T(8,128)(2,1)S(1)}, u32[]{:S(2)}, u32[]{:S(2)}) collective-permute-start(bf16[32,2048]{1,0:T(8,128)(2,1)S(1)} %scale.1.refs_0_), channel_id=1, source_target_pairs={{0,64},{32,96},{64,0},{96,32},{1,65},{33,97},{65,1},{97,33},{2,66}... | collective-permute-start | bytes 393224 | tf_op jit(solution)/shard_map/ppermute | solution.py:171
  40.6 1.3 %collective-permute-start.2 = (bf16[32,2048]{1,0:T(8,128)(2,1)S(1)}, bf16[32,2048]{1,0:T(8,128)(2,1)S(1)}, u32[]{:S(2)}, u32[]{:S(2)}) collective-permute-start(bf16[32,2048]{1,0:T(8,128)(2,1)S(1)} %scale.1.refs_0_), channel_id=1, source_target_pairs={{0,96},{32,0},{64,32},{96,64},{1,97},{33,1},{65,33},{97,65},{2,98}... | collective-permute-start | bytes 393224 | tf_op jit(solution)/shard_map/ppermute | solution.py:171
  41.9 0.2 collective-permute-start.1
  42.1 0.5 collective-permute-start
  42.6 2.9 %collective-permute-start.8 = (bf16[32,2048]{1,0:T(8,128)(2,1)S(1)}, bf16[32,2048]{1,0:T(8,128)(2,1)S(1)}, u32[]{:S(2)}, u32[]{:S(2)}) collective-permute-start(bf16[32,2048]{1,0:T(8,128)(2,1)S(1)} %scale.1.refs_0_), channel_id=1, source_target_pairs={{0,16},{16,0},{1,17},{17,1},{2,18},{18,2},{3,19},{19,3},{4,20},{20... | collective-permute-start | bytes 393224 | tf_op jit(solution)/shard_map/ppermute | solution.py:167
  45.5 0.0 collective-permute-done.3.refs_0_
  45.5 1.0 %collective-permute-done.2.refs_6_ = bf16[32,2048]{1,0:T(8,128)(2,1)S(1)} collective-permute-done((bf16[32,2048]{1,0:T(8,128)(2,1)S(1)}, bf16[32,2048]{1,0:T(8,128)(2,1)S(1)}, u32[]{:S(2)}, u32[]{:S(2)}) %collective-permute-start.2) | collective-permute-done | bytes 131104 | tf_op jit(solution)/shard_map/ppermute | solution.py:171
  46.5 2.3 %collective-permute-done.1.refs_4_ = bf16[32,2048]{1,0:T(8,128)(2,1)S(1)} collective-permute-done((bf16[32,2048]{1,0:T(8,128)(2,1)S(1)}, bf16[32,2048]{1,0:T(8,128)(2,1)S(1)}, u32[]{:S(2)}, u32[]{:S(2)}) %collective-permute-start.1) | collective-permute-done | bytes 131104 | tf_op jit(solution)/shard_map/ppermute | solution.py:171
  48.8 0.0 collective-permute-done.refs_2_
  48.8 1.6 %collective-permute-start.9 = (bf16[32,2048]{1,0:T(8,128)(2,1)S(1)}, bf16[32,2048]{1,0:T(8,128)(2,1)S(1)}, u32[]{:S(2)}, u32[]{:S(2)}) collective-permute-start(bf16[32,2048]{1,0:T(8,128)(2,1)S(1)} %collective-permute-done.refs_2_), channel_id=1, source_target_pairs={{0,16},{16,0},{1,17},{17,1},{2,18},{18,2},{3,19},{19,3},{4,20},{20... | collective-permute-start | bytes 393224 | tf_op jit(solution)/shard_map/ppermute | solution.py:167
  50.4 0.0 collective-permute-start.10
  50.4 0.5 collective-permute-start.11
  50.9 0.5 collective-permute-start.7
  51.4 0.0 collective-permute-done.8.refs_1_
  51.5 0.9 %collective-permute-start.5 = (bf16[32,2048]{1,0:T(8,128)(2,1)S(1)}, bf16[32,2048]{1,0:T(8,128)(2,1)S(1)}, u32[]{:S(2)}, u32[]{:S(2)}) collective-permute-start(bf16[32,2048]{1,0:T(8,128)(2,1)S(1)} %collective-permute-done.1.refs_4_), channel_id=1, source_target_pairs={{0,128},{128,0},{1,129},{129,1},{2,130},{130,2},{3,131},{131,3},{4... | collective-permute-start | bytes 393224 | tf_op jit(solution)/shard_map/ppermute | solution.py:167
  52.4 0.0 collective-permute-done.9.refs_3_
  52.4 1.3 %collective-permute-start.6 = (bf16[32,2048]{1,0:T(8,128)(2,1)S(1)}, bf16[32,2048]{1,0:T(8,128)(2,1)S(1)}, u32[]{:S(2)}, u32[]{:S(2)}) collective-permute-start(bf16[32,2048]{1,0:T(8,128)(2,1)S(1)} %collective-permute-done.refs_2_), channel_id=1, source_target_pairs={{0,96},{32,0},{64,32},{96,64},{1,97},{33,1},{65,33},{97,65},{2,98}... | collective-permute-start | bytes 393224 | tf_op jit(solution)/shard_map/ppermute | solution.py:171
  53.7 0.0 collective-permute-done.10.refs_5_
  53.7 0.8 %collective-permute-start.4 = (bf16[32,2048]{1,0:T(8,128)(2,1)S(1)}, bf16[32,2048]{1,0:T(8,128)(2,1)S(1)}, u32[]{:S(2)}, u32[]{:S(2)}) collective-permute-start(bf16[32,2048]{1,0:T(8,128)(2,1)S(1)} %collective-permute-done.3.refs_0_), channel_id=1, source_target_pairs={{0,16},{16,0},{1,17},{17,1},{2,18},{18,2},{3,19},{19,3},{4,20},{20... | collective-permute-start | bytes 393224 | tf_op jit(solution)/shard_map/ppermute | solution.py:167
  54.5 0.0 collective-permute-done.11.refs_7_
  54.5 3.4 %near.1.refs_9_ = f32[1,512,2048]{2,1,0:T(8,128)} custom-call(bf16[32,2048]{1,0:T(8,128)(2,1)S(1)} %scale.1.refs_0_, bf16[32,2048]{1,0:T(8,128)(2,1)S(1)} %collective-permute-done.8.refs_1_, bf16[32,2048]{1,0:T(8,128)(2,1)S(1)} %collective-permute-done.refs_2_, bf16[32,2048]{1,0:T(8,128)(2,1)S(1)} %collective-permute-done.9.refs_3_, ...), custom_call_target="tpu_custom_call" | custom-call | tf_op jit(solution)/shard_map/near/pallas_call | solution.py:177
  57.9 0.0 collective-permute-done.7.refs_6_
  57.9 0.9 %collective-permute-done.5.refs_2_ = bf16[32,2048]{1,0:T(8,128)(2,1)S(1)} collective-permute-done((bf16[32,2048]{1,0:T(8,128)(2,1)S(1)}, bf16[32,2048]{1,0:T(8,128)(2,1)S(1)}, u32[]{:S(2)}, u32[]{:S(2)}) %collective-permute-start.5) | collective-permute-done | bytes 131104 | tf_op jit(solution)/shard_map/ppermute | solution.py:167
  58.9 0.0 collective-permute-done.6.refs_4_
  58.9 0.8 %collective-permute-start.12 = (bf16[32,2048]{1,0:T(8,128)(2,1)S(1)}, bf16[32,2048]{1,0:T(8,128)(2,1)S(1)}, u32[]{:S(2)}, u32[]{:S(2)}) collective-permute-start(bf16[32,2048]{1,0:T(8,128)(2,1)S(1)} %collective-permute-done.5.refs_2_), channel_id=1, source_target_pairs={{0,16},{16,0},{1,17},{17,1},{2,18},{18,2},{3,19},{19,3},{4,20},{20... | collective-permute-start | bytes 393224 | tf_op jit(solution)/shard_map/ppermute | solution.py:167
  59.6 0.0 collective-permute-start.13
  59.6 0.5 collective-permute-start.14
  60.2 0.0 collective-permute-done.4.refs_1_
  60.2 0.5 collective-permute-done.12.refs_3_
  60.6 0.4 collective-permute-done.13.refs_5_
  61.0 0.2 collective-permute-done.14.refs_7_
  61.2 3.4 %far.1 = f32[1,512,2048]{2,1,0:T(8,128)} custom-call(bf16[32,2048]{1,0:T(8,128)(2,1)S(1)} %collective-permute-done.3.refs_0_, bf16[32,2048]{1,0:T(8,128)(2,1)S(1)} %collective-permute-done.4.refs_1_, bf16[32,2048]{1,0:T(8,128)(2,1)S(1)} %collective-permute-done.5.refs_2_, ...), custom_call_target="tpu_custom_call", output_to_operand_aliasing={{}: (9, {})} | custom-call | tf_op jit(solution)/shard_map/far/pallas_call | solution.py:177
Async XLA Ops:
  39.4 6.1 %collective-permute-start.3 = (bf16[32,2048]{1,0:T(8,128)(2,1)S(1)}, bf16[32,2048]{1,0:T(8,128)(2,1)S(1)}, u32[]{:S(2)}, u32[]{:S(2)}) collective-permute-start(bf16[32,2048]{1,0:T(8,128)(2,1)S(1)} %scale.1.refs_0_), channel_id=1, source_target_pairs={{0,64},{32,96},{64,0},{96,32},{1,65},{33,97},{65,1},{97,33},{2,66}... | collective-permute-start | bytes 393224 | tf_op jit(solution)/shard_map/ppermute | solution.py:171
  40.6 5.9 %collective-permute-start.2 = (bf16[32,2048]{1,0:T(8,128)(2,1)S(1)}, bf16[32,2048]{1,0:T(8,128)(2,1)S(1)}, u32[]{:S(2)}, u32[]{:S(2)}) collective-permute-start(bf16[32,2048]{1,0:T(8,128)(2,1)S(1)} %scale.1.refs_0_), channel_id=1, source_target_pairs={{0,96},{32,0},{64,32},{96,64},{1,97},{33,1},{65,33},{97,65},{2,98}... | collective-permute-start | bytes 393224 | tf_op jit(solution)/shard_map/ppermute | solution.py:171
  41.9 7.0 %collective-permute-start.1 = (bf16[32,2048]{1,0:T(8,128)(2,1)S(1)}, bf16[32,2048]{1,0:T(8,128)(2,1)S(1)}, u32[]{:S(2)}, u32[]{:S(2)}) collective-permute-start(bf16[32,2048]{1,0:T(8,128)(2,1)S(1)} %scale.1.refs_0_), channel_id=1, source_target_pairs={{0,32},{32,64},{64,96},{96,0},{1,33},{33,65},{65,97},{97,1},{2,34}... | collective-permute-start | bytes 393224 | tf_op jit(solution)/shard_map/ppermute | solution.py:171
  42.1 6.8 %collective-permute-start = (bf16[32,2048]{1,0:T(8,128)(2,1)S(1)}, bf16[32,2048]{1,0:T(8,128)(2,1)S(1)}, u32[]{:S(2)}, u32[]{:S(2)}) collective-permute-start(bf16[32,2048]{1,0:T(8,128)(2,1)S(1)} %scale.1.refs_0_), channel_id=1, source_target_pairs={{0,128},{128,0},{1,129},{129,1},{2,130},{130,2},{3,131},{131,3},{4... | collective-permute-start | bytes 393224 | tf_op jit(solution)/shard_map/ppermute | solution.py:167
  42.6 8.9 %collective-permute-start.8 = (bf16[32,2048]{1,0:T(8,128)(2,1)S(1)}, bf16[32,2048]{1,0:T(8,128)(2,1)S(1)}, u32[]{:S(2)}, u32[]{:S(2)}) collective-permute-start(bf16[32,2048]{1,0:T(8,128)(2,1)S(1)} %scale.1.refs_0_), channel_id=1, source_target_pairs={{0,16},{16,0},{1,17},{17,1},{2,18},{18,2},{3,19},{19,3},{4,20},{20... | collective-permute-start | bytes 393224 | tf_op jit(solution)/shard_map/ppermute | solution.py:167
  48.8 3.6 %collective-permute-start.9 = (bf16[32,2048]{1,0:T(8,128)(2,1)S(1)}, bf16[32,2048]{1,0:T(8,128)(2,1)S(1)}, u32[]{:S(2)}, u32[]{:S(2)}) collective-permute-start(bf16[32,2048]{1,0:T(8,128)(2,1)S(1)} %collective-permute-done.refs_2_), channel_id=1, source_target_pairs={{0,16},{16,0},{1,17},{17,1},{2,18},{18,2},{3,19},{19,3},{4,20},{20... | collective-permute-start | bytes 393224 | tf_op jit(solution)/shard_map/ppermute | solution.py:167
  50.4 3.3 %collective-permute-start.10 = (bf16[32,2048]{1,0:T(8,128)(2,1)S(1)}, bf16[32,2048]{1,0:T(8,128)(2,1)S(1)}, u32[]{:S(2)}, u32[]{:S(2)}) collective-permute-start(bf16[32,2048]{1,0:T(8,128)(2,1)S(1)} %collective-permute-done.1.refs_4_), channel_id=1, source_target_pairs={{0,16},{16,0},{1,17},{17,1},{2,18},{18,2},{3,19},{19,3},{4,20},{20... | collective-permute-start | bytes 393224 | tf_op jit(solution)/shard_map/ppermute | solution.py:167
  50.4 4.1 %collective-permute-start.11 = (bf16[32,2048]{1,0:T(8,128)(2,1)S(1)}, bf16[32,2048]{1,0:T(8,128)(2,1)S(1)}, u32[]{:S(2)}, u32[]{:S(2)}) collective-permute-start(bf16[32,2048]{1,0:T(8,128)(2,1)S(1)} %collective-permute-done.2.refs_6_), channel_id=1, source_target_pairs={{0,16},{16,0},{1,17},{17,1},{2,18},{18,2},{3,19},{19,3},{4,20},{20... | collective-permute-start | bytes 393224 | tf_op jit(solution)/shard_map/ppermute | solution.py:167
  50.9 7.0 %collective-permute-start.7 = (bf16[32,2048]{1,0:T(8,128)(2,1)S(1)}, bf16[32,2048]{1,0:T(8,128)(2,1)S(1)}, u32[]{:S(2)}, u32[]{:S(2)}) collective-permute-start(bf16[32,2048]{1,0:T(8,128)(2,1)S(1)} %collective-permute-done.3.refs_0_), channel_id=1, source_target_pairs={{0,128},{128,0},{1,129},{129,1},{2,130},{130,2},{3,131},{131,3},{4... | collective-permute-start | bytes 393224 | tf_op jit(solution)/shard_map/ppermute | solution.py:167
  51.5 7.4 %collective-permute-start.5 = (bf16[32,2048]{1,0:T(8,128)(2,1)S(1)}, bf16[32,2048]{1,0:T(8,128)(2,1)S(1)}, u32[]{:S(2)}, u32[]{:S(2)}) collective-permute-start(bf16[32,2048]{1,0:T(8,128)(2,1)S(1)} %collective-permute-done.1.refs_4_), channel_id=1, source_target_pairs={{0,128},{128,0},{1,129},{129,1},{2,130},{130,2},{3,131},{131,3},{4... | collective-permute-start | bytes 393224 | tf_op jit(solution)/shard_map/ppermute | solution.py:167
  52.4 6.5 %collective-permute-start.6 = (bf16[32,2048]{1,0:T(8,128)(2,1)S(1)}, bf16[32,2048]{1,0:T(8,128)(2,1)S(1)}, u32[]{:S(2)}, u32[]{:S(2)}) collective-permute-start(bf16[32,2048]{1,0:T(8,128)(2,1)S(1)} %collective-permute-done.refs_2_), channel_id=1, source_target_pairs={{0,96},{32,0},{64,32},{96,64},{1,97},{33,1},{65,33},{97,65},{2,98}... | collective-permute-start | bytes 393224 | tf_op jit(solution)/shard_map/ppermute | solution.py:171
  53.7 6.5 %collective-permute-start.4 = (bf16[32,2048]{1,0:T(8,128)(2,1)S(1)}, bf16[32,2048]{1,0:T(8,128)(2,1)S(1)}, u32[]{:S(2)}, u32[]{:S(2)}) collective-permute-start(bf16[32,2048]{1,0:T(8,128)(2,1)S(1)} %collective-permute-done.3.refs_0_), channel_id=1, source_target_pairs={{0,16},{16,0},{1,17},{17,1},{2,18},{18,2},{3,19},{19,3},{4,20},{20... | collective-permute-start | bytes 393224 | tf_op jit(solution)/shard_map/ppermute | solution.py:167
  58.9 1.8 %collective-permute-start.12 = (bf16[32,2048]{1,0:T(8,128)(2,1)S(1)}, bf16[32,2048]{1,0:T(8,128)(2,1)S(1)}, u32[]{:S(2)}, u32[]{:S(2)}) collective-permute-start(bf16[32,2048]{1,0:T(8,128)(2,1)S(1)} %collective-permute-done.5.refs_2_), channel_id=1, source_target_pairs={{0,16},{16,0},{1,17},{17,1},{2,18},{18,2},{3,19},{19,3},{4,20},{20... | collective-permute-start | bytes 393224 | tf_op jit(solution)/shard_map/ppermute | solution.py:167
  59.6 1.3 %collective-permute-start.13 = (bf16[32,2048]{1,0:T(8,128)(2,1)S(1)}, bf16[32,2048]{1,0:T(8,128)(2,1)S(1)}, u32[]{:S(2)}, u32[]{:S(2)}) collective-permute-start(bf16[32,2048]{1,0:T(8,128)(2,1)S(1)} %collective-permute-done.6.refs_4_), channel_id=1, source_target_pairs={{0,16},{16,0},{1,17},{17,1},{2,18},{18,2},{3,19},{19,3},{4,20},{20... | collective-permute-start | bytes 393224 | tf_op jit(solution)/shard_map/ppermute | solution.py:167
  59.6 1.5 %collective-permute-start.14 = (bf16[32,2048]{1,0:T(8,128)(2,1)S(1)}, bf16[32,2048]{1,0:T(8,128)(2,1)S(1)}, u32[]{:S(2)}, u32[]{:S(2)}) collective-permute-start(bf16[32,2048]{1,0:T(8,128)(2,1)S(1)} %collective-permute-done.7.refs_6_), channel_id=1, source_target_pairs={{0,16},{16,0},{1,17},{17,1},{2,18},{18,2},{3,19},{19,3},{4,20},{20... | collective-permute-start | bytes 393224 | tf_op jit(solution)/shard_map/ppermute | solution.py:167

commit v5 on v4

--- a/solution.py
+++ b/solution.py
@@ -18,6 +18,7 @@
 LANES = OWN * MOST
 F = G * A
 TILE = 512
+REST = 256
 BF = jnp.bfloat16
 F32 = jnp.float32
 NT = (((1,), (1,)), ((), ()))
@@ -36,7 +37,7 @@
 
 def slot_kernel(act_hbm, grad_hbm, ids_hbm, own_hbm, po_hbm, pi_hbm, train_hbm, send_ref, po_ref, pi_ref, train_ref,
                 act_ref, grad_ref, ids_ref, own_ref, sem):
-    sources = (ids_hbm, own_hbm, act_hbm, grad_hbm, po_hbm, pi_hbm, train_hbm)
+    sources = (ids_hbm, own_hbm, act_hbm, grad_hbm, po_hbm, pi_hbm, train_hbm.at[:, : train_ref.shape[1]])
     targets = (ids_ref, own_ref, act_ref, grad_ref, po_ref, pi_ref, train_ref)
     copies = [pltpu.make_async_copy(a, b, sem.at[i]) for i, (a, b) in enumerate(zip(sources, targets))]
     for copy in copies:
@@ -83,7 +84,9 @@
     return jnp.dot(a, b, preferred_element_type=F32)
 
 
-def cond_kernel(recv_ref, po_ref, pi_ref, cond_ref, square_ref):
+def cond_kernel(recv_ref, po_ref, pi_ref, train_hbm, cond_ref, square_ref, rest_ref, sem):
+    copy = pltpu.make_async_copy(train_hbm.at[:, train_hbm.shape[1] - REST :], rest_ref, sem)
+    copy.start()
     span = OWN // 4
     wide = BLK * span * MOST
     mask = (iota((span * A, wide), 0) // A) == (iota((span * A, wide), 1) // MOST % span)
@@ -125,6 +128,7 @@
     row = jnp.transpose(jnp.broadcast_to(square, (OWN, 128)))[:8]
     row = jnp.concatenate([row, jnp.zeros((8, 128 - OWN), F32)], axis=1)
     square_ref[...] = jnp.concatenate([row] * (BLK // 8), axis=0)
+    copy.wait()
 
 
 def scale_kernel(cond_ref, squares_ref, doc_ref):
@@ -154,13 +158,15 @@
         copy.wait()
 
 
-def tiles_of(train_ref):
-    return [lambda i=i: train_ref[0, i * TILE : (i + 1) * TILE] for i in range(train_ref.shape[1] // TILE)]
+def tiles_of(train_ref, rest_ref):
+    full = train_ref.shape[1] // TILE
+    tiles = [lambda i=i: train_ref[0, i * TILE : (i + 1) * TILE] for i in range(full)]
+    return tiles + [lambda: jnp.concatenate([train_ref[0, full * TILE :], rest_ref[0]], axis=0)]
 
 
 def score_kernel(places, count, *refs):
-    blocks, train_ref, (out_hbm, buffer, sem) = refs[:count], refs[count], refs[-3:]
-    score_tiles(places, blocks, tiles_of(train_ref), out_hbm, buffer, sem)
+    blocks, trains, (out_hbm, buffer, sem) = refs[:count], refs[count : count + 2], refs[-3:]
+    score_tiles(places, blocks, tiles_of(*trains), out_hbm, buffer, sem)
 
 
 def swap(x, axis):
@@ -173,20 +179,20 @@
 
 def score(places, blocks, train, *out):
     hbm = pl.BlockSpec(memory_space=pltpu.HBM)
-    rows = train.shape[1]
+    rows = sum(t.shape[1] for t in train)
     return pl.pallas_call(
         functools.partial(score_kernel, places, len(blocks)),
         out_shape=pltpu.HBM((1, DOCS, rows), F32),
-        in_specs=[VM] * (len(blocks) + 1) + [hbm] * len(out),
+        in_specs=[VM] * (len(blocks) + 2) + [hbm] * len(out),
         out_specs=hbm,
         scratch_shapes=[
             pltpu.VMEM((len(places) * OWN, rows), F32),
             pltpu.SemaphoreType.DMA((rows // TILE, len(places))),
         ],
-        input_output_aliases={len(blocks) + 1: 0} if out else {},
+        input_output_aliases={len(blocks) + 2: 0} if out else {},
         name="far" if out else "near",
         compiler_params=room(8),
-    )(*blocks, train, *out)
+    )(*blocks, *train, *out)
 
 
 def pair(block):
@@ -200,13 +206,15 @@
 def body(act, grad, train, pre_out, pre_in, doc_ids, owners):
     hbm = pl.BlockSpec(memory_space=pltpu.HBM)
     ids, own = doc_ids.reshape(1, TOK), owners.reshape(1, DOCS)
+    train = pltpu.with_memory_space_constraint(train, pltpu.HBM)
     kept = (pre_out, pre_in, train)
     loaded = (act, grad, ids, own)
-    send, pre_out, pre_in, train = pl.pallas_call(
+    send, pre_out, pre_in, first = pl.pallas_call(
         slot_kernel,
         out_shape=(
             jax.ShapeDtypeStruct((BLK, W, LANES), BF),
-            *(pltpu.VMEM(v.shape, v.dtype) for v in kept),
+            *(pltpu.VMEM(v.shape, v.dtype) for v in kept[:2]),
+            pltpu.VMEM((1, train.shape[1] - REST, F), BF),
         ),
         in_specs=[hbm] * 7,
         out_specs=[VM] * 4,
@@ -216,19 +224,21 @@
         ],
         name="slots",
         compiler_params=room(24),
-    )(*(pltpu.with_memory_space_constraint(v, pltpu.HBM) for v in (*loaded, *kept)))
+    )(*(pltpu.with_memory_space_constraint(v, pltpu.HBM) for v in (*loaded, *kept[:2])), train)
     received = lax.all_to_all(send, BLK_AXES, split_axis=0, concat_axis=0, tiled=True)
-    cond, squares = pl.pallas_call(
+    cond, squares, rest = pl.pallas_call(
         cond_kernel,
         out_shape=(
             jax.ShapeDtypeStruct((OWN, F), F32),
             jax.ShapeDtypeStruct((BLK, 128), F32),
+            pltpu.VMEM((1, REST, F), BF),
         ),
-        in_specs=[VM] * 3,
-        out_specs=[VM] * 2,
+        in_specs=[VM] * 3 + [hbm],
+        out_specs=[VM] * 3,
+        scratch_shapes=[pltpu.SemaphoreType.DMA],
         name="condition",
         compiler_params=room(16),
-    )(received, pre_out, pre_in)
+    )(received, pre_out, pre_in, train)
     squares = lax.all_to_all(squares, MOD_AXES, split_axis=0, concat_axis=0, tiled=True)
     doc = pl.pallas_call(
         scale_kernel,
@@ -238,6 +248,7 @@
         name="scale",
         compiler_params=room(2),
     )(cond, squares)
+    train = (first, rest)
     side, above, below, over = swap(doc, "xl"), turn(doc, 1), turn(doc, -1), turn(doc, 2)
     side_above, side_below, side_over = swap(above, "xl"), turn(side, -1), swap(over, "xl")
     side, above, below, over = lax.optimization_barrier((side, above, below, over))

time: 65 us -> 65.7 us (1.011)
  Pallas kernels: 12.1 us -> 12.8 us
    pallas_call x1, Pallas kernels: 1.47 us -> 2.5 us  [body(): pl.pallas_call(cond_kernel, out_shape=(jax.ShapeDtypeStruct((OWN, F), F32...]
where the time goes in v5:
time: 65.7 us; the launch traced here: 65.5 us
  blocking collectives  34.2 us (52%)
  starting transfers between devices  13 us (20%)
  Pallas kernels  12.8 us (19%)
  waiting for transfers between devices  5.25 us (8%)
    all_to_all x1, blocking collectives, body(): lax.all_to_all(squares, MOD_AXES, split_axis=0, concat_axis=0, tiled=True)  19.1 us
    all_to_all x1, blocking collectives, body(): lax.all_to_all(send, BLK_AXES, split_axis=0, concat_axis=0, tiled=True)  15.1 us
    ppermute x11, starting transfers between devices, swap(): return lax.ppermute(x, axis, [(0, 1), (1, 0)])  9.14 us
    pallas_call x2, Pallas kernels, score(): pl.pallas_call(functools.partial(score_kernel, places, len(blocks)), out_...  6.85 us
    ppermute x4, starting transfers between devices, turn(): return lax.ppermute(x, 'y', [(i, (i + by) % 4) for i in range(4)])  3.89 us
    pallas_call x1, Pallas kernels, body(): pl.pallas_call(slot_kernel, out_shape=(jax.ShapeDtypeStruct((BLK, W, LANE...  3.33 us
    ppermute x4, waiting for transfers between devices, turn(): return lax.ppermute(x, 'y', [(i, (i + by) % 4) for i in range(4)])  3.3 us
    pallas_call x1, Pallas kernels, body(): pl.pallas_call(cond_kernel, out_shape=(jax.ShapeDtypeStruct((OWN, F), F32...  2.5 us
  transfers between devices with their start and end apart: 15, of which 6 were waited for; matrix products, arithmetic and copies ran while one was open for 0% of the time, Pallas kernels for 5%

profile of v5, /device:TPU:1, one launch (start us, length us, event | category | flops | bytes accessed | tf_op | source)
XLA Modules:
  0.0 65.5 jit_solution(364241536058926851)
XLA Ops:
  0.0 3.3 %slots.1 = (bf16[16,96,128]{2,1,0:T(8,128)(2,1)S(1)}, f32[1,64,64]{2,1,0:T(8,128)S(1)}, f32[1,32,32]{2,1,0:T(8,128)S(1)}, bf16[1,1792,2048]{2,1,0:T(8,128)(2,1)S(1)}) custom-call(bf16[1,32,1024]{2,1,0:T(8,128)(2,1)} %act_hbm.1, bf16[1,64,1024]{2,1,0:T(8,128)(2,1)} %grad_hbm.1, s32[1,1024]{1,0:T(1,128)} %bitcast.8, s32[1,512]{1,0:T(1,128)} %bitcast.9, ...), custom_call_target="tpu_custom_call" | custom-call | tf_op jit(solution)/shard_map/slots/pallas_call | solution.py:212
  3.3 15.1 %all_to_all.16.recv_ref = bf16[16,96,128]{2,1,0:T(8,128)(2,1)S(1)} all-to-all(bf16[16,96,128]{2,1,0:T(8,128)(2,1)S(1)} %get-tuple-element.20), channel_id=1, replica_groups=mesh['xl'=2,'y'=4,'core'=2,'xh'=2,'z'=8] {'xl','y','core'}, dimensions={0} | all-to-all | bytes 786432 | tf_op jit(solution)/shard_map/all_to_all | solution.py:228
  18.4 2.5 %condition.1 = (f32[32,2048]{1,0:T(8,128)S(1)}, f32[16,128]{1,0:T(8,128)S(1)}, bf16[1,256,2048]{2,1,0:T(8,128)(2,1)S(1)}) custom-call(bf16[16,96,128]{2,1,0:T(8,128)(2,1)S(1)} %all_to_all.16.recv_ref, f32[1,64,64]{2,1,0:T(8,128)S(1)} %get-tuple-element.21.po_ref, f32[1,32,32]{2,1,0:T(8,128)S(1)} %get-tuple-element.22.pi_ref, bf16[1,2048,2048]{2,1,0:T(8,128)(2,1)} %train_hbm.3), custom_call_target="tpu_custom_call" | custom-call | tf_op jit(solution)/shard_map/condition/pallas_call | solution.py:229
  20.9 19.1 %all_to_all.17 = f32[16,1,128]{2,1,0:T(1,128)S(1)} all-to-all(f32[16,1,128]{2,1,0:T(1,128)S(1)} %bitcast.7), channel_id=1, replica_groups=mesh['xl'=2,'y'=4,'core'=2,'xh'=2,'z'=8] {'xh','z'}, dimensions={0} | all-to-all | bytes 16384 | tf_op jit(solution)/shard_map/all_to_all | solution.py:242
  40.0 0.2 scale.1.refs_0_
  40.2 1.2 %collective-permute-start.3 = (bf16[32,2048]{1,0:T(8,128)(2,1)S(1)}, bf16[32,2048]{1,0:T(8,128)(2,1)S(1)}, u32[]{:S(2)}, u32[]{:S(2)}) collective-permute-start(bf16[32,2048]{1,0:T(8,128)(2,1)S(1)} %scale.1.refs_0_), channel_id=1, source_target_pairs={{0,64},{32,96},{64,0},{96,32},{1,65},{33,97},{65,1},{97,33},{2,66}... | collective-permute-start | bytes 393224 | tf_op jit(solution)/shard_map/ppermute | solution.py:177
  41.4 1.3 %collective-permute-start.2 = (bf16[32,2048]{1,0:T(8,128)(2,1)S(1)}, bf16[32,2048]{1,0:T(8,128)(2,1)S(1)}, u32[]{:S(2)}, u32[]{:S(2)}) collective-permute-start(bf16[32,2048]{1,0:T(8,128)(2,1)S(1)} %scale.1.refs_0_), channel_id=1, source_target_pairs={{0,96},{32,0},{64,32},{96,64},{1,97},{33,1},{65,33},{97,65},{2,98}... | collective-permute-start | bytes 393224 | tf_op jit(solution)/shard_map/ppermute | solution.py:177
  42.6 0.2 collective-permute-start.1
  42.8 0.5 collective-permute-start
  43.3 2.9 %collective-permute-start.8 = (bf16[32,2048]{1,0:T(8,128)(2,1)S(1)}, bf16[32,2048]{1,0:T(8,128)(2,1)S(1)}, u32[]{:S(2)}, u32[]{:S(2)}) collective-permute-start(bf16[32,2048]{1,0:T(8,128)(2,1)S(1)} %scale.1.refs_0_), channel_id=1, source_target_pairs={{0,16},{16,0},{1,17},{17,1},{2,18},{18,2},{3,19},{19,3},{4,20},{20... | collective-permute-start | bytes 393224 | tf_op jit(solution)/shard_map/ppermute | solution.py:173
  46.3 0.0 collective-permute-done.3.refs_0_
  46.3 1.0 %collective-permute-done.2.refs_6_ = bf16[32,2048]{1,0:T(8,128)(2,1)S(1)} collective-permute-done((bf16[32,2048]{1,0:T(8,128)(2,1)S(1)}, bf16[32,2048]{1,0:T(8,128)(2,1)S(1)}, u32[]{:S(2)}, u32[]{:S(2)}) %collective-permute-start.2) | collective-permute-done | bytes 131104 | tf_op jit(solution)/shard_map/ppermute | solution.py:177
  47.3 2.3 %collective-permute-done.1.refs_4_ = bf16[32,2048]{1,0:T(8,128)(2,1)S(1)} collective-permute-done((bf16[32,2048]{1,0:T(8,128)(2,1)S(1)}, bf16[32,2048]{1,0:T(8,128)(2,1)S(1)}, u32[]{:S(2)}, u32[]{:S(2)}) %collective-permute-start.1) | collective-permute-done | bytes 131104 | tf_op jit(solution)/shard_map/ppermute | solution.py:177
  49.6 0.0 collective-permute-done.refs_2_
  49.6 1.6 %collective-permute-start.9 = (bf16[32,2048]{1,0:T(8,128)(2,1)S(1)}, bf16[32,2048]{1,0:T(8,128)(2,1)S(1)}, u32[]{:S(2)}, u32[]{:S(2)}) collective-permute-start(bf16[32,2048]{1,0:T(8,128)(2,1)S(1)} %collective-permute-done.refs_2_), channel_id=1, source_target_pairs={{0,16},{16,0},{1,17},{17,1},{2,18},{18,2},{3,19},{19,3},{4,20},{20... | collective-permute-start | bytes 393224 | tf_op jit(solution)/shard_map/ppermute | solution.py:173
  51.1 0.0 collective-permute-start.10
  51.2 0.5 collective-permute-start.11
  51.7 0.5 collective-permute-start.7
  52.2 0.0 collective-permute-done.8.refs_1_
  52.2 0.9 %collective-permute-start.5 = (bf16[32,2048]{1,0:T(8,128)(2,1)S(1)}, bf16[32,2048]{1,0:T(8,128)(2,1)S(1)}, u32[]{:S(2)}, u32[]{:S(2)}) collective-permute-start(bf16[32,2048]{1,0:T(8,128)(2,1)S(1)} %collective-permute-done.1.refs_4_), channel_id=1, source_target_pairs={{0,128},{128,0},{1,129},{129,1},{2,130},{130,2},{3,131},{131,3},{4... | collective-permute-start | bytes 393224 | tf_op jit(solution)/shard_map/ppermute | solution.py:173
  53.1 0.0 collective-permute-done.9.refs_3_
  53.1 1.3 %collective-permute-start.6 = (bf16[32,2048]{1,0:T(8,128)(2,1)S(1)}, bf16[32,2048]{1,0:T(8,128)(2,1)S(1)}, u32[]{:S(2)}, u32[]{:S(2)}) collective-permute-start(bf16[32,2048]{1,0:T(8,128)(2,1)S(1)} %collective-permute-done.refs_2_), channel_id=1, source_target_pairs={{0,96},{32,0},{64,32},{96,64},{1,97},{33,1},{65,33},{97,65},{2,98}... | collective-permute-start | bytes 393224 | tf_op jit(solution)/shard_map/ppermute | solution.py:177
  54.4 0.0 collective-permute-done.10.refs_5_
  54.4 0.8 %collective-permute-start.4 = (bf16[32,2048]{1,0:T(8,128)(2,1)S(1)}, bf16[32,2048]{1,0:T(8,128)(2,1)S(1)}, u32[]{:S(2)}, u32[]{:S(2)}) collective-permute-start(bf16[32,2048]{1,0:T(8,128)(2,1)S(1)} %collective-permute-done.3.refs_0_), channel_id=1, source_target_pairs={{0,16},{16,0},{1,17},{17,1},{2,18},{18,2},{3,19},{19,3},{4,20},{20... | collective-permute-start | bytes 393224 | tf_op jit(solution)/shard_map/ppermute | solution.py:173
  55.2 0.0 collective-permute-done.11.refs_7_
  55.2 3.4 %near.1.refs_10_ = f32[1,512,2048]{2,1,0:T(8,128)} custom-call(bf16[32,2048]{1,0:T(8,128)(2,1)S(1)} %scale.1.refs_0_, bf16[32,2048]{1,0:T(8,128)(2,1)S(1)} %collective-permute-done.8.refs_1_, bf16[32,2048]{1,0:T(8,128)(2,1)S(1)} %collective-permute-done.refs_2_, bf16[32,2048]{1,0:T(8,128)(2,1)S(1)} %collective-permute-done.9.refs_3_, ...), custom_call_target="tpu_custom_call" | custom-call | tf_op jit(solution)/shard_map/near/pallas_call | solution.py:183
  58.7 0.0 collective-permute-done.7.refs_6_
  58.7 0.9 %collective-permute-done.5.refs_2_ = bf16[32,2048]{1,0:T(8,128)(2,1)S(1)} collective-permute-done((bf16[32,2048]{1,0:T(8,128)(2,1)S(1)}, bf16[32,2048]{1,0:T(8,128)(2,1)S(1)}, u32[]{:S(2)}, u32[]{:S(2)}) %collective-permute-start.5) | collective-permute-done | bytes 131104 | tf_op jit(solution)/shard_map/ppermute | solution.py:173
  59.6 0.0 collective-permute-done.6.refs_4_
  59.6 0.8 %collective-permute-start.12 = (bf16[32,2048]{1,0:T(8,128)(2,1)S(1)}, bf16[32,2048]{1,0:T(8,128)(2,1)S(1)}, u32[]{:S(2)}, u32[]{:S(2)}) collective-permute-start(bf16[32,2048]{1,0:T(8,128)(2,1)S(1)} %collective-permute-done.5.refs_2_), channel_id=1, source_target_pairs={{0,16},{16,0},{1,17},{17,1},{2,18},{18,2},{3,19},{19,3},{4,20},{20... | collective-permute-start | bytes 393224 | tf_op jit(solution)/shard_map/ppermute | solution.py:173
  60.4 0.0 collective-permute-start.13
  60.4 0.5 collective-permute-start.14
  60.9 0.0 collective-permute-done.4.refs_1_
  60.9 0.5 collective-permute-done.12.refs_3_
  61.4 0.4 collective-permute-done.13.refs_5_
  61.7 0.2 collective-permute-done.14.refs_7_
  61.9 3.4 %far.1 = f32[1,512,2048]{2,1,0:T(8,128)} custom-call(bf16[32,2048]{1,0:T(8,128)(2,1)S(1)} %collective-permute-done.3.refs_0_, bf16[32,2048]{1,0:T(8,128)(2,1)S(1)} %collective-permute-done.4.refs_1_, bf16[32,2048]{1,0:T(8,128)(2,1)S(1)} %collective-permute-done.5.refs_2_, ...), custom_call_target="tpu_custom_call", output_to_operand_aliasing={{}: (10, {})} | custom-call | tf_op jit(solution)/shard_map/far/pallas_call | solution.py:183
Async XLA Ops:
  40.2 6.1 %collective-permute-start.3 = (bf16[32,2048]{1,0:T(8,128)(2,1)S(1)}, bf16[32,2048]{1,0:T(8,128)(2,1)S(1)}, u32[]{:S(2)}, u32[]{:S(2)}) collective-permute-start(bf16[32,2048]{1,0:T(8,128)(2,1)S(1)} %scale.1.refs_0_), channel_id=1, source_target_pairs={{0,64},{32,96},{64,0},{96,32},{1,65},{33,97},{65,1},{97,33},{2,66}... | collective-permute-start | bytes 393224 | tf_op jit(solution)/shard_map/ppermute | solution.py:177
  41.4 5.9 %collective-permute-start.2 = (bf16[32,2048]{1,0:T(8,128)(2,1)S(1)}, bf16[32,2048]{1,0:T(8,128)(2,1)S(1)}, u32[]{:S(2)}, u32[]{:S(2)}) collective-permute-start(bf16[32,2048]{1,0:T(8,128)(2,1)S(1)} %scale.1.refs_0_), channel_id=1, source_target_pairs={{0,96},{32,0},{64,32},{96,64},{1,97},{33,1},{65,33},{97,65},{2,98}... | collective-permute-start | bytes 393224 | tf_op jit(solution)/shard_map/ppermute | solution.py:177
  42.6 7.0 %collective-permute-start.1 = (bf16[32,2048]{1,0:T(8,128)(2,1)S(1)}, bf16[32,2048]{1,0:T(8,128)(2,1)S(1)}, u32[]{:S(2)}, u32[]{:S(2)}) collective-permute-start(bf16[32,2048]{1,0:T(8,128)(2,1)S(1)} %scale.1.refs_0_), channel_id=1, source_target_pairs={{0,32},{32,64},{64,96},{96,0},{1,33},{33,65},{65,97},{97,1},{2,34}... | collective-permute-start | bytes 393224 | tf_op jit(solution)/shard_map/ppermute | solution.py:177
  42.8 6.8 %collective-permute-start = (bf16[32,2048]{1,0:T(8,128)(2,1)S(1)}, bf16[32,2048]{1,0:T(8,128)(2,1)S(1)}, u32[]{:S(2)}, u32[]{:S(2)}) collective-permute-start(bf16[32,2048]{1,0:T(8,128)(2,1)S(1)} %scale.1.refs_0_), channel_id=1, source_target_pairs={{0,128},{128,0},{1,129},{129,1},{2,130},{130,2},{3,131},{131,3},{4... | collective-permute-start | bytes 393224 | tf_op jit(solution)/shard_map/ppermute | solution.py:173
  43.3 8.9 %collective-permute-start.8 = (bf16[32,2048]{1,0:T(8,128)(2,1)S(1)}, bf16[32,2048]{1,0:T(8,128)(2,1)S(1)}, u32[]{:S(2)}, u32[]{:S(2)}) collective-permute-start(bf16[32,2048]{1,0:T(8,128)(2,1)S(1)} %scale.1.refs_0_), channel_id=1, source_target_pairs={{0,16},{16,0},{1,17},{17,1},{2,18},{18,2},{3,19},{19,3},{4,20},{20... | collective-permute-start | bytes 393224 | tf_op jit(solution)/shard_map/ppermute | solution.py:173
  49.6 3.6 %collective-permute-start.9 = (bf16[32,2048]{1,0:T(8,128)(2,1)S(1)}, bf16[32,2048]{1,0:T(8,128)(2,1)S(1)}, u32[]{:S(2)}, u32[]{:S(2)}) collective-permute-start(bf16[32,2048]{1,0:T(8,128)(2,1)S(1)} %collective-permute-done.refs_2_), channel_id=1, source_target_pairs={{0,16},{16,0},{1,17},{17,1},{2,18},{18,2},{3,19},{19,3},{4,20},{20... | collective-permute-start | bytes 393224 | tf_op jit(solution)/shard_map/ppermute | solution.py:173
  51.1 3.2 %collective-permute-start.10 = (bf16[32,2048]{1,0:T(8,128)(2,1)S(1)}, bf16[32,2048]{1,0:T(8,128)(2,1)S(1)}, u32[]{:S(2)}, u32[]{:S(2)}) collective-permute-start(bf16[32,2048]{1,0:T(8,128)(2,1)S(1)} %collective-permute-done.1.refs_4_), channel_id=1, source_target_pairs={{0,16},{16,0},{1,17},{17,1},{2,18},{18,2},{3,19},{19,3},{4,20},{20... | collective-permute-start | bytes 393224 | tf_op jit(solution)/shard_map/ppermute | solution.py:173
  51.2 4.1 %collective-permute-start.11 = (bf16[32,2048]{1,0:T(8,128)(2,1)S(1)}, bf16[32,2048]{1,0:T(8,128)(2,1)S(1)}, u32[]{:S(2)}, u32[]{:S(2)}) collective-permute-start(bf16[32,2048]{1,0:T(8,128)(2,1)S(1)} %collective-permute-done.2.refs_6_), channel_id=1, source_target_pairs={{0,16},{16,0},{1,17},{17,1},{2,18},{18,2},{3,19},{19,3},{4,20},{20... | collective-permute-start | bytes 393224 | tf_op jit(solution)/shard_map/ppermute | solution.py:173
  51.7 7.0 %collective-permute-start.7 = (bf16[32,2048]{1,0:T(8,128)(2,1)S(1)}, bf16[32,2048]{1,0:T(8,128)(2,1)S(1)}, u32[]{:S(2)}, u32[]{:S(2)}) collective-permute-start(bf16[32,2048]{1,0:T(8,128)(2,1)S(1)} %collective-permute-done.3.refs_0_), channel_id=1, source_target_pairs={{0,128},{128,0},{1,129},{129,1},{2,130},{130,2},{3,131},{131,3},{4... | collective-permute-start | bytes 393224 | tf_op jit(solution)/shard_map/ppermute | solution.py:173
  52.2 7.4 %collective-permute-start.5 = (bf16[32,2048]{1,0:T(8,128)(2,1)S(1)}, bf16[32,2048]{1,0:T(8,128)(2,1)S(1)}, u32[]{:S(2)}, u32[]{:S(2)}) collective-permute-start(bf16[32,2048]{1,0:T(8,128)(2,1)S(1)} %collective-permute-done.1.refs_4_), channel_id=1, source_target_pairs={{0,128},{128,0},{1,129},{129,1},{2,130},{130,2},{3,131},{131,3},{4... | collective-permute-start | bytes 393224 | tf_op jit(solution)/shard_map/ppermute | solution.py:173
  53.1 6.5 %collective-permute-start.6 = (bf16[32,2048]{1,0:T(8,128)(2,1)S(1)}, bf16[32,2048]{1,0:T(8,128)(2,1)S(1)}, u32[]{:S(2)}, u32[]{:S(2)}) collective-permute-start(bf16[32,2048]{1,0:T(8,128)(2,1)S(1)} %collective-permute-done.refs_2_), channel_id=1, source_target_pairs={{0,96},{32,0},{64,32},{96,64},{1,97},{33,1},{65,33},{97,65},{2,98}... | collective-permute-start | bytes 393224 | tf_op jit(solution)/shard_map/ppermute | solution.py:177
  54.4 6.5 %collective-permute-start.4 = (bf16[32,2048]{1,0:T(8,128)(2,1)S(1)}, bf16[32,2048]{1,0:T(8,128)(2,1)S(1)}, u32[]{:S(2)}, u32[]{:S(2)}) collective-permute-start(bf16[32,2048]{1,0:T(8,128)(2,1)S(1)} %collective-permute-done.3.refs_0_), channel_id=1, source_target_pairs={{0,16},{16,0},{1,17},{17,1},{2,18},{18,2},{3,19},{19,3},{4,20},{20... | collective-permute-start | bytes 393224 | tf_op jit(solution)/shard_map/ppermute | solution.py:173
  59.6 1.8 %collective-permute-start.12 = (bf16[32,2048]{1,0:T(8,128)(2,1)S(1)}, bf16[32,2048]{1,0:T(8,128)(2,1)S(1)}, u32[]{:S(2)}, u32[]{:S(2)}) collective-permute-start(bf16[32,2048]{1,0:T(8,128)(2,1)S(1)} %collective-permute-done.5.refs_2_), channel_id=1, source_target_pairs={{0,16},{16,0},{1,17},{17,1},{2,18},{18,2},{3,19},{19,3},{4,20},{20... | collective-permute-start | bytes 393224 | tf_op jit(solution)/shard_map/ppermute | solution.py:173
  60.4 1.3 %collective-permute-start.13 = (bf16[32,2048]{1,0:T(8,128)(2,1)S(1)}, bf16[32,2048]{1,0:T(8,128)(2,1)S(1)}, u32[]{:S(2)}, u32[]{:S(2)}) collective-permute-start(bf16[32,2048]{1,0:T(8,128)(2,1)S(1)} %collective-permute-done.6.refs_4_), channel_id=1, source_target_pairs={{0,16},{16,0},{1,17},{17,1},{2,18},{18,2},{3,19},{19,3},{4,20},{20... | collective-permute-start | bytes 393224 | tf_op jit(solution)/shard_map/ppermute | solution.py:173
  60.4 1.5 %collective-permute-start.14 = (bf16[32,2048]{1,0:T(8,128)(2,1)S(1)}, bf16[32,2048]{1,0:T(8,128)(2,1)S(1)}, u32[]{:S(2)}, u32[]{:S(2)}) collective-permute-start(bf16[32,2048]{1,0:T(8,128)(2,1)S(1)} %collective-permute-done.7.refs_6_), channel_id=1, source_target_pairs={{0,16},{16,0},{1,17},{17,1},{2,18},{18,2},{3,19},{19,3},{4,20},{20... | collective-permute-start | bytes 393224 | tf_op jit(solution)/shard_map/ppermute | solution.py:173
